TPU v7x, 512 devices: a whole 4x8x8 slice. The times are simulated.
512 devices in a mesh: seq: 64 (over y_lo, z, core), head: 8 (over x, y_hi).
Axes of the slice: x: 4, y: 8 (y_hi: 2, y_lo: 4; y = y_hi * 4 + y_lo), z: 8, core: 2. Of those that a mesh axis runs over, the one named last changes fastest.
Arguments:
- query_rows: bfloat16 [20480, 3072], P('seq', 'head'), may hold values from -6 to 6
- key_rows: bfloat16 [20480, 3072], P('seq', 'head'), may hold values from -6 to 6
- value_rows: bfloat16 [20480, 3072], P('seq', 'head'), may hold values from -6 to 6
- pattern: int32 [64, 6], P('seq'), may hold values 0 or 1
- owners: int32 [4], replicated, may hold values from 0 to 63, as said below
- out_weight: bfloat16 [3072, 3072], P('head'), may hold values from -0.15625 to 0.15625
Outputs:
- mixed: bfloat16 [20480, 3072], P('seq', 'head')
Inputs may be any that keep to these rules, and one draw needn't show every extreme that they name: `owners`: distinct block indices; blocks 0 and 64 - 1 are always among them.
All inputs are finite; a program needn't handle non-finite values. No bound on the sum of `pattern` on one device may be relied on, other than what follows from the above.
Results may differ from a plain program's by a relative error of at most 0.02.
Values may be sent and summed in bfloat16 or wider, within the bound.
A program may use at most 64 MiB of HBM per device.

v0:
```python
import jax
import jax.numpy as jnp
from jax import lax
from jax.sharding import PartitionSpec as P

HD = 128
REACH = 3
OWNERS = 4
REF_DEV = 256


def broadcast(block, axis, owner):
    block = jnp.where(lax.axis_index(axis) == owner, block, jnp.zeros_like(block))
    return lax.psum(block, axis)


def from_behind(value, axis, steps):
    count = lax.axis_size(axis)
    pairs = [(source, (source + steps) % count) for source in range(count)]
    return lax.ppermute(value, axis, pairs)


def column_of(offset):
    return offset + REACH if offset < 0 else offset + REACH - 1


def merge_block(state, query_three, block_keys, block_values):
    peaks, totals, summed_values = state
    local_heads = query_three.shape[1]
    keys_three = block_keys.reshape(-1, local_heads, HD)
    values_three = block_values.reshape(-1, local_heads, HD)
    scores = jnp.einsum(
        "qhd,khd->hqk", query_three, keys_three, preferred_element_type=jnp.float32
    ) * HD ** (-0.5)
    new_peaks = jnp.maximum(peaks, jnp.max(scores, axis=-1))
    rescale = jnp.exp(peaks - new_peaks)
    weights = jnp.exp(scores - new_peaks[:, :, None])
    totals = totals * rescale + jnp.sum(weights, axis=-1)
    contrib = jnp.einsum(
        "hqk,khd->hqd",
        weights.astype(jnp.bfloat16),
        values_three,
        preferred_element_type=jnp.float32,
    )
    summed_values = summed_values * rescale[:, :, None] + contrib
    return (new_peaks, totals, summed_values)


def absorb(state, query_three, stacked, active):
    return lax.cond(
        active,
        lambda inner: merge_block(inner, query_three, stacked[0], stacked[1]),
        lambda inner: inner,
        state,
    )


def body(query_rows, key_rows, value_rows, pattern, owners, out_weight):
    row_count = query_rows.shape[0]
    local_width = query_rows.shape[1]
    local_heads = local_width // HD
    query_three = query_rows.reshape(row_count, local_heads, HD)
    start_state = (
        jnp.full((local_heads, row_count), -jnp.inf, jnp.float32),
        jnp.zeros((local_heads, row_count), jnp.float32),
        jnp.zeros((local_heads, row_count, HD), jnp.float32),
    )
    state = merge_block(start_state, query_three, key_rows, value_rows)
    own_stack = jnp.stack([key_rows, value_rows])
    ref_stack = jnp.stack([key_rows[:REF_DEV], value_rows[:REF_DEV]])
    for member in range(OWNERS):
        arrived = broadcast(ref_stack, "seq", owners[member])
        state = merge_block(state, query_three, arrived[0], arrived[1])
    for distance in range(1, REACH + 1):
        for offset in (-distance, distance):
            arrived = from_behind(own_stack, "seq", -offset)
            state = absorb(state, query_three, arrived, pattern[0, column_of(offset)] != 0)
    peaks, totals, summed_values = state
    attended = summed_values / totals[:, :, None]
    attended = (
        jnp.transpose(attended, (1, 0, 2)).reshape(row_count, local_width).astype(jnp.bfloat16)
    )
    partial_value = jnp.dot(attended, out_weight, preferred_element_type=jnp.float32)
    return lax.psum_scatter(
        partial_value.astype(jnp.bfloat16), "head", scatter_dimension=1, tiled=True
    )


def solution(mesh):
    return jax.shard_map(
        body,
        mesh=mesh,
        in_specs=(
            P("seq", "head"),
            P("seq", "head"),
            P("seq", "head"),
            P("seq", None),
            P(),
            P("head", None),
        ),
        out_specs=P("seq", "head"),
        check_vma=False,
    )
```

profile of v0, /device:TPU:1, one launch (start us, length us, event | category | flops | bytes accessed | tf_op | source)
XLA Modules:
  0.0 710.8 jit_solution(8907911057021929676)
XLA Ops:
  6.5 1.5 fusion.78
  8.1 1.2 copy.87
  9.2 1.2 copy.83
  13.0 1.2 broadcast_select_fusion
  14.3 1.8 pad_maximum_fusion
  16.0 5.4 collective-permute-start
  21.4 5.3 collective-permute-start.1
  26.8 1.9 collective-permute-start.2
  28.7 8.3 %collective-permute-start.3 = (bf16[2,320,384]{2,1,0:T(8,128)(2,1)}, bf16[2,320,384]{2,1,0:T(8,128)(2,1)}, u32[]{:S(2)}, u32[]{:S(2)}) collective-permute-start(bf16[2,320,384]{2,1,0:T(8,128)(2,1)} %pad_maximum_fusion), channel_id=1, source_target_pairs={{0,496},{8,504},{16,0},{24,8},{32,16},{40,24},{48,32},{56,40},{64,... | collective-permute-start | bytes 1474568 | tf_op jit(solution)/shard_map/ppermute | solution.py:20
  37.0 1.9 collective-permute-start.4
  43.4 1.2 copy.82
  45.0 1.1 copy-done.1
  46.4 519.6 %all-reduce.3.cloned.1.call-done = (bf16[2,256,384]{1,2,0:T(8,128)(2,1)}, bf16[2,256,384]{1,2,0:T(8,128)(2,1)}, bf16[2,256,384]{1,2,0:T(8,128)(2,1)}, bf16[2,256,384]{1,2,0:T(8,128)(2,1)}) async-done(((bf16[2,256,384]{1,2,0:T(8,128)(2,1)}, bf16[2,256,384]{1,2,0:T(8,128)(2,1)}, bf16[2,256,384]{1,2,0:T(8,128)(2,1)}, bf16[2,256,384]{1,2,0:T(8,128)(2,1)}), (bf16[2,256,384]{1,2,0:T(8,128)(2,1)}, ...) | async-done | bytes 1572880 | tf_op jit(solution)/shard_map/psum | solution.py:14
  566.0 1.1 fusion.77
  572.7 6.7 collective-permute-start.5
  579.4 1.3 fusion.37
  580.7 4.6 conditional.6
  580.7 2.1 copy.103
  582.8 1.1 fusion.62
  585.4 4.8 conditional.9
  585.6 2.1 copy.109
  587.6 1.1 fusion.68
  590.1 4.6 conditional.10
  590.2 2.1 copy.111
  592.2 1.1 fusion.70
  594.7 4.6 conditional.11
  594.7 2.1 copy.113
  596.8 1.1 fusion.72
  599.7 2.5 convolution_convert_fusion
  602.2 4.1 copy.156
  606.3 95.9 %reduce-scatter.4.cloned.1.call-done = bf16[384,320]{1,0:T(8,128)(2,1)} async-done(((bf16[3072,320]{1,0:T(8,128)(2,1)}), bf16[384,320]{1,0:T(8,128)(2,1)}) %reduce-scatter.4.cloned.1.call-update) | async-done | bytes 245776
  702.2 1.8 copy.157
  (73 shorter events, 12.8 us)
Async XLA Ops:
  6.5 593.2 %copy-start = (bf16[384,3072]{1,0:T(8,128)(2,1)S(1)}, bf16[384,3072]{1,0:T(8,128)(2,1)}, u32[]{:S(2)}) copy-start(bf16[384,3072]{1,0:T(8,128)(2,1)} %param.23) | copy-start | bytes 7077892
  6.5 559.5 %all-reduce.3.cloned.1.call-start = ((), (), s32[]{:S(2)}) async-start(), calls=%async_computation.2 | async-start | bytes 3145728 | tf_op jit(solution)/shard_map/psum | solution.py:14
  12.9 1.3 copy-start.3
  14.2 24.8 %copy-start.7 = (s32[1,6]{1,0:T(1,128)S(1)}, s32[1,6]{1,0:T(1,128)}, u32[]{:S(2)}) copy-start(s32[1,6]{1,0:T(1,128)} %param.21) | copy-start | bytes 76
  14.2 688.0 %reduce-scatter.4.cloned.1.call-start = ((), (), s32[]{:S(2)}) async-start(), calls=%async_computation.1 | async-start | bytes 2654208
  16.0 556.7 %collective-permute-start = (bf16[2,320,384]{2,1,0:T(8,128)(2,1)}, bf16[2,320,384]{2,1,0:T(8,128)(2,1)}, u32[]{:S(2)}, u32[]{:S(2)}) collective-permute-start(bf16[2,320,384]{2,1,0:T(8,128)(2,1)} %pad_maximum_fusion), channel_id=1, source_target_pairs={{0,8},{8,16},{16,24},{24,32},{32,40},{40,48},{48,56},{56,64},{64,7... | collective-permute-start | bytes 1474568 | tf_op jit(solution)/shard_map/ppermute | solution.py:20
  21.4 563.9 %collective-permute-start.1 = (bf16[2,320,384]{2,1,0:T(8,128)(2,1)}, bf16[2,320,384]{2,1,0:T(8,128)(2,1)}, u32[]{:S(2)}, u32[]{:S(2)}) collective-permute-start(bf16[2,320,384]{2,1,0:T(8,128)(2,1)} %pad_maximum_fusion), channel_id=1, source_target_pairs={{0,504},{8,0},{16,8},{24,16},{32,24},{40,32},{48,40},{56,48},{64,5... | collective-permute-start | bytes 1474568 | tf_op jit(solution)/shard_map/ppermute | solution.py:20
  26.8 558.6 %collective-permute-start.2 = (bf16[2,320,384]{2,1,0:T(8,128)(2,1)}, bf16[2,320,384]{2,1,0:T(8,128)(2,1)}, u32[]{:S(2)}, u32[]{:S(2)}) collective-permute-start(bf16[2,320,384]{2,1,0:T(8,128)(2,1)} %pad_maximum_fusion), channel_id=1, source_target_pairs={{0,16},{8,24},{16,32},{24,40},{32,48},{40,56},{48,64},{56,72},{64,... | collective-permute-start | bytes 1474568 | tf_op jit(solution)/shard_map/ppermute | solution.py:20
  28.7 556.7 %collective-permute-start.3 = (bf16[2,320,384]{2,1,0:T(8,128)(2,1)}, bf16[2,320,384]{2,1,0:T(8,128)(2,1)}, u32[]{:S(2)}, u32[]{:S(2)}) collective-permute-start(bf16[2,320,384]{2,1,0:T(8,128)(2,1)} %pad_maximum_fusion), channel_id=1, source_target_pairs={{0,496},{8,504},{16,0},{24,8},{32,16},{40,24},{48,32},{56,40},{64,... | collective-permute-start | bytes 1474568 | tf_op jit(solution)/shard_map/ppermute | solution.py:20
  37.0 553.1 %collective-permute-start.4 = (bf16[2,320,384]{2,1,0:T(8,128)(2,1)}, bf16[2,320,384]{2,1,0:T(8,128)(2,1)}, u32[]{:S(2)}, u32[]{:S(2)}) collective-permute-start(bf16[2,320,384]{2,1,0:T(8,128)(2,1)} %pad_maximum_fusion), channel_id=1, source_target_pairs={{0,24},{8,32},{16,40},{24,48},{32,56},{40,64},{48,72},{56,80},{64,... | collective-permute-start | bytes 1474568 | tf_op jit(solution)/shard_map/ppermute | solution.py:20
  45.0 1.1 copy-start.1
  566.0 1.6 copy-start.6
  567.6 1.0 copy-start.5
  568.1 1.0 copy-start.4
  572.0 7.4 %copy-start.2 = (f32[3,320,320]{1,2,0:T(8,128)S(1)}, f32[3,320,320]{1,2,0:T(8,128)}, u32[]{:S(2)}) copy-start(f32[3,320,320]{1,2,0:T(8,128)} %copy-done.1) | copy-start | bytes 3686404
  572.7 22.0 %collective-permute-start.5 = (bf16[2,320,384]{2,1,0:T(8,128)(2,1)}, bf16[2,320,384]{2,1,0:T(8,128)(2,1)}, u32[]{:S(2)}, u32[]{:S(2)}) collective-permute-start(bf16[2,320,384]{2,1,0:T(8,128)(2,1)} %pad_maximum_fusion), channel_id=1, source_target_pairs={{0,488},{8,496},{16,504},{24,0},{32,8},{40,16},{48,24},{56,32},{64... | collective-permute-start | bytes 1474568 | tf_op jit(solution)/shard_map/ppermute | solution.py:20
Sparse Core Ops, SparseCore 0:
  14.3 551.6 all-reduce.2
  606.4 95.6 reduce-scatter.3
where the time goes:
time: 712 us; the launch traced here: 711 us
  waiting for transfers between devices  616 us (87%)
  starting transfers between devices  29.6 us (4%)
  local copies, waits for them, and re-layouts  27.4 us (4%)
  between operations  20 us (3%)
  matrix products  11.8 us (2%)
    psum x1, waiting for transfers between devices, broadcast(): return lax.psum(block, axis)  520 us
    unnamed x3, waiting for transfers between devices  95.9 us
    ppermute x6, starting transfers between devices, from_behind(): return lax.ppermute(value, axis, pairs)  29.6 us
  transfers between devices with their start and end apart: 8, of which 2 were waited for; matrix products, arithmetic and copies ran while one was open for 4% of the time, Pallas kernels for 0%

commit v1 on v0

v1 whole, which is shorter than its diff:
```python
import functools

import jax
import jax.numpy as jnp
from jax import lax
from jax.experimental import pallas as pl
from jax.experimental.pallas import tpu as pltpu
from jax.sharding import PartitionSpec as P

MESH = pl.DeviceIdType.MESH
HD = 128
LH = 3
TOK = 320
REF = 256
REACH = 3
NZ = 8
NY = 4
NX = 4
HK = 2 * LH
CH = 2
OWN = 4 * REF
HALO = OWN + TOK
KEYS = HALO + 2 * REACH * TOK
PAD = -(-KEYS // 256) * 256
NEG = -1e30
VMEM = pl.BlockSpec(memory_space=pltpu.VMEM)
SMEM = pl.BlockSpec(memory_space=pltpu.SMEM)
BF = jnp.bfloat16


def gather_kernel(
    owners_ref, k_ref, v_ref, kv, mine, stat, msend, mrecv, zp_s, zp_r, zs_s, zs_r,
    yp_s, yp_r, ys_s, ys_r, hs_sem, hr_sem, rs_sem, rr_sem,
):
    s = lax.axis_index("seq")
    n = 2 * NZ * NY
    core = lax.rem(s, 2)
    z = lax.rem(s // 2, NZ)
    y = s // (2 * NZ)
    step = 1 - 2 * core
    pz = jnp.where(core == 0, z, NZ - 1 - z)
    py = jnp.where(core == 0, y, NY - 1 - y)
    right = lax.rem(s + 2, n)
    left = lax.rem(s - 2 + n, n)
    partner = s + step
    extra = lax.rem(s - step + n, n)
    znext = lax.rem(s + 2 * step + n, n)
    zprev = lax.rem(s - 2 * step + n, n)
    ynext = lax.rem(s + 2 * NZ * step + n, n)
    yprev = lax.rem(s - 2 * NZ * step + n, n)

    barrier = pltpu.get_barrier_semaphore()
    for peer in (partner, right, left, extra, ynext, yprev):
        pl.semaphore_signal(barrier, inc=1, device_id={"seq": peer}, device_id_type=MESH)

    for h in range(LH):
        cols = slice(h * HD, (h + 1) * HD)
        kv[2 * h, OWN:HALO, :] = k_ref[:, cols]
        kv[2 * h + 1, OWN:HALO, :] = v_ref[:, cols]
    if PAD > KEYS:
        kv[:, KEYS:PAD, :] = jnp.zeros((HK, PAD - KEYS, HD), BF)

    low = jnp.int32(n)
    high = jnp.int32(-1)
    for i in range(4):
        o = owners_ref[i]
        low = jnp.minimum(low, jnp.where(o == 0, n, o))
        high = jnp.maximum(high, jnp.where(o == n - 1, -1, o))
    wanted = jnp.where(core == 0, low, high)
    given = jnp.where(core == 0, high, low)
    keep = jnp.where(wanted == s, 1.0, 0.0).astype(BF)
    give = jnp.where(given == s, 1.0, 0.0).astype(BF)
    fixed = jnp.where((pz == 0) & (py == 0), 1.0, 0.0).astype(BF)
    rows = REF // CH
    for hk in range(HK):
        for c in range(CH):
            block = kv[hk, OWN + c * rows : OWN + (c + 1) * rows, :]
            mine[hk * CH + c] = block * keep
            msend[hk * CH + c] = block * give
            stat[hk * CH + c] = block * fixed

    @pl.when(pz == 0)
    def _():
        zp_r[...] = jnp.zeros_like(zp_r)

    @pl.when(pz == NZ - 1)
    def _():
        zs_r[...] = jnp.zeros_like(zs_r)

    @pl.when(py == 0)
    def _():
        yp_r[...] = jnp.zeros_like(yp_r)

    @pl.when(py == NY - 1)
    def _():
        ys_r[...] = jnp.zeros_like(ys_r)

    pl.semaphore_wait(barrier, 6)
    chunks = HK * CH

    def ref_copy(kind, src, dst, k, peer):
        return pltpu.make_async_remote_copy(
            src_ref=src, dst_ref=dst, send_sem=rs_sem.at[kind, k], recv_sem=rr_sem.at[kind, k],
            device_id={"seq": peer}, device_id_type=MESH,
        )

    def m_copy(k):
        return ref_copy(0, msend.at[k], mrecv.at[k], k, partner)

    def zp_copy(k):
        return ref_copy(1, zp_s.at[k], zp_r.at[k], k, znext)

    def zs_copy(k):
        return ref_copy(2, zs_s.at[k], zs_r.at[k], k, zprev)

    def yp_copy(k):
        return ref_copy(3, yp_s.at[k], yp_r.at[k], k, ynext)

    def ys_copy(k):
        return ref_copy(4, ys_s.at[k], ys_r.at[k], k, yprev)

    def ref_rows(k, slot):
        return kv.at[k // CH, pl.ds(pl.multiple_of(slot * REF + lax.rem(k, CH) * rows, rows), rows)]

    def fx_copy(k):
        place = ref_rows(k, core)
        return ref_copy(5, place, place, k, partner)

    def fs_copy(k):
        place = ref_rows(k, 2 + core)
        return ref_copy(6, place, place, k, partner)

    def fx_wait(k):
        place = ref_rows(k, 1 - core)
        ref_copy(5, place, place, k, partner).wait_recv()

    def fs_wait(k):
        place = ref_rows(k, 3 - core)
        ref_copy(6, place, place, k, partner).wait_recv()

    def halo_rows(hk, col):
        return kv.at[hk, pl.ds(pl.multiple_of(HALO + col * TOK, 16), TOK)]

    def halo_copy(kind, src, hk, col, peer):
        return pltpu.make_async_remote_copy(
            src_ref=src, dst_ref=halo_rows(hk, col), send_sem=hs_sem.at[kind, hk],
            recv_sem=hr_sem.at[col, hk], device_id={"seq": peer}, device_id_type=MESH,
        )

    def own_rows(hk):
        return kv.at[hk, OWN:HALO]

    def halo_sends(hk):
        return (
            halo_copy(0, own_rows(hk), hk, 1, right),
            halo_copy(1, own_rows(hk), hk, 4, left),
            halo_copy(2, own_rows(hk), hk, 2 + core, partner),
        )

    def forward_behind(hk):
        return halo_copy(3, halo_rows(hk, 1), hk, 2 * core, partner)

    def forward_ahead(hk):
        return halo_copy(4, halo_rows(hk, 4), hk, 3 + 2 * core, partner)

    def forward_far(hk):
        return halo_copy(5, halo_rows(hk, 4 - 3 * core), hk, 5 - 5 * core, extra)

    def halo_wait(hk, col):
        halo_copy(0, own_rows(hk), hk, col, right).wait_recv()

    def start_m(k, carry):
        m_copy(k).start()
        return carry

    lax.fori_loop(0, chunks, start_m, 0)

    def when_in(k, bound, body):
        @pl.when((k >= 0) & (k < bound))
        def _():
            body(k)

    def zs_step(k):
        @pl.when(pz < NZ - 1)
        def _():
            zs_copy(k).wait_recv()

        @pl.when(pz > 0)
        def _():
            zs_s[k] = zs_r[k] + mine[k]
            zs_copy(k).start()

    def z_total(k):
        mine[k] = mine[k] + zp_r[k, 0] + zs_r[k]
        stat[k] = stat[k] + zp_r[k, 1]

    def yp_step(k):
        @pl.when(py > 0)
        def _():
            yp_copy(k).wait_recv()

        @pl.when(py < NY - 1)
        def _():
            yp_s[k, 0] = yp_r[k, 0] + mine[k]
            yp_s[k, 1] = yp_r[k, 1] + stat[k]
            yp_copy(k).start()

    def ys_step(k):
        @pl.when(py < NY - 1)
        def _():
            ys_copy(k).wait_recv()

        @pl.when(py > 0)
        def _():
            ys_s[k] = ys_r[k] + mine[k]
            ys_copy(k).start()

    def last_step(k):
        ref_rows(k, core)[...] = mine[k] + yp_r[k, 0] + ys_r[k]
        ref_rows(k, 2 + core)[...] = stat[k] + yp_r[k, 1]
        fx_copy(k).start()
        fs_copy(k).start()

    def halo_start(hk):
        for copy in halo_sends(hk):
            copy.start()

    def halo_forward(hk):
        halo_wait(hk, 1)
        halo_wait(hk, 4)
        forward_behind(hk).start()
        forward_ahead(hk).start()
        forward_far(hk).start()

    lag = NZ - 1

    def tick(t, carry):
        when_in(t - pz, chunks, zp_step_guarded)
        when_in(t - (NZ - 1 - pz), chunks, zs_step_guarded)
        when_in(t - lag, chunks, z_total)
        when_in(t - lag - py, chunks, yp_step)
        when_in(t - lag - (NY - 1 - py), chunks, ys_step)
        when_in(t - lag - (NY - 1), chunks, last_step)
        when_in(jnp.where(lax.rem(t, 2) == 0, t // 2, -1), HK, halo_start)
        when_in(jnp.where(lax.rem(t, 2) == 0, t // 2 - 2, -1), HK, halo_forward)
        return carry

    def merged(k):
        m_copy(k).wait_recv()
        mine[k] = mine[k] + mrecv[k]

    primary_first = pz <= NZ - 1 - pz

    def zp_step_guarded(k):
        @pl.when(primary_first)
        def _():
            merged(k)

        @pl.when(pz > 0)
        def _():
            zp_copy(k).wait_recv()

        @pl.when(pz < NZ - 1)
        def _():
            zp_s[k, 0] = zp_r[k, 0] + mine[k]
            zp_s[k, 1] = zp_r[k, 1] + stat[k]
            zp_copy(k).start()

    def zs_step_guarded(k):
        @pl.when(jnp.logical_not(primary_first))
        def _():
            merged(k)

        zs_step(k)

    lax.fori_loop(0, chunks + lag + NY - 1, tick, 0)

    def finish_ref(k, carry):
        fx_wait(k)
        fs_wait(k)
        m_copy(k).wait_send()
        fx_copy(k).wait_send()
        fs_copy(k).wait_send()

        @pl.when(pz < NZ - 1)
        def _():
            zp_copy(k).wait_send()

        @pl.when(pz > 0)
        def _():
            zs_copy(k).wait_send()

        @pl.when(py < NY - 1)
        def _():
            yp_copy(k).wait_send()

        @pl.when(py > 0)
        def _():
            ys_copy(k).wait_send()

        return carry

    lax.fori_loop(0, chunks, finish_ref, 0)

    def finish(hk, carry):
        for col in (0, 2, 3, 5):
            halo_wait(hk, col)
        for copy in halo_sends(hk):
            copy.wait_send()
        forward_behind(hk).wait_send()
        forward_ahead(hk).wait_send()
        forward_far(hk).wait_send()
        return carry

    lax.fori_loop(0, HK, finish, 0)


def gather(owners, k, v):
    chunks = HK * CH
    rows = REF // CH
    dma = pltpu.SemaphoreType.DMA
    one = pltpu.VMEM((chunks, rows, HD), BF)
    two = pltpu.VMEM((chunks, 2, rows, HD), BF)
    return pl.pallas_call(
        gather_kernel,
        out_shape=jax.ShapeDtypeStruct((HK, PAD, HD), BF),
        in_specs=[SMEM, VMEM, VMEM],
        out_specs=VMEM,
        scratch_shapes=[
            one, one, one, one, two, two, one, one, two, two, one, one,
            dma((6, HK)), dma((6, HK)), dma((7, chunks)), dma((7, chunks)),
        ],
        compiler_params=pltpu.CompilerParams(
            collective_id=0, has_side_effects=True, vmem_limit_bytes=40 << 20
        ),
        name="gather_keys",
    )(owners, k, v)


def attend_kernel(pattern_ref, q_ref, kv, w_ref, out, scores, att):
    position = lax.broadcasted_iota(jnp.int32, (1, PAD), 1)
    bias = jnp.where(position >= KEYS, NEG, 0.0)
    for col in range(2 * REACH):
        low = HALO + col * TOK
        closed = jnp.where(pattern_ref[0, col] != 0, 0.0, NEG)
        bias = bias + jnp.where((position >= low) & (position < low + TOK), closed, 0.0)
    scale = HD ** -0.5
    for h in range(LH):
        q = q_ref[:, h * HD : (h + 1) * HD]
        peak = jnp.full((TOK, HD), NEG, jnp.float32)
        for t in range(PAD // 256):
            keys = kv[2 * h, t * 256 : (t + 1) * 256, :]
            sc = lax.dot_general(
                q, keys, (((1,), (1,)), ((), ())), preferred_element_type=jnp.float32
            )
            sc = sc * scale + bias[:, t * 256 : (t + 1) * 256]
            scores[:, t * 256 : (t + 1) * 256] = sc
            peak = jnp.maximum(peak, jnp.maximum(sc[:, :128], sc[:, 128:]))
        top = jnp.max(peak, axis=1, keepdims=True)
        total = jnp.zeros((TOK, HD), jnp.float32)
        acc = jnp.zeros((TOK, HD), jnp.float32)
        for t in range(PAD // 256):
            w = jnp.exp(scores[:, t * 256 : (t + 1) * 256] - top)
            total = total + (w[:, :128] + w[:, 128:])
            acc = acc + jnp.dot(
                w.astype(BF), kv[2 * h + 1, t * 256 : (t + 1) * 256, :],
                preferred_element_type=jnp.float32,
            )
        total = jnp.sum(total, axis=1, keepdims=True)
        att[:, h * HD : (h + 1) * HD] = (acc / total).astype(BF)
    width = LH * HD
    for b in range(2 * NX):
        out[b] = jnp.dot(
            att[...], w_ref[:, b * width : (b + 1) * width], preferred_element_type=jnp.float32
        ).astype(BF)


def attend(pattern, q, kv, w):
    return pl.pallas_call(
        attend_kernel,
        out_shape=jax.ShapeDtypeStruct((2 * NX, TOK, LH * HD), BF),
        in_specs=[SMEM, VMEM, VMEM, VMEM],
        out_specs=VMEM,
        scratch_shapes=[pltpu.VMEM((TOK, PAD), jnp.float32), pltpu.VMEM((TOK, LH * HD), BF)],
        compiler_params=pltpu.CompilerParams(vmem_limit_bytes=48 << 20),
        name="attend",
    )(pattern, q, kv, w)


def mix_kernel(p, out, r1p, r1m, t2p, t2m, r2p, r2m, ty, ry, s_sem, r_sem, y_sem):
    h = lax.axis_index("head")
    x = h // 2
    y = lax.rem(h, 2)
    xn = lax.rem(x + 1, NX)
    xp = lax.rem(x + NX - 1, NX)
    xo = lax.rem(x + 2, NX)
    nxt = xn * 2 + y
    prv = xp * 2 + y
    pair = x * 2 + 1 - y
    barrier = pltpu.get_barrier_semaphore()
    for peer in (nxt, prv, pair):
        pl.semaphore_signal(barrier, inc=1, device_id={"head": peer}, device_id_type=MESH)
    pl.semaphore_wait(barrier, 3)
    half = TOK // 2
    top, bottom = slice(0, half), slice(half, TOK)

    def copy(kind, i, src, dst, peer):
        return pltpu.make_async_remote_copy(
            src_ref=src, dst_ref=dst, send_sem=s_sem.at[kind, i], recv_sem=r_sem.at[kind, i],
            device_id={"head": peer}, device_id_type=MESH,
        )

    def cross(i):
        return pltpu.make_async_remote_copy(
            src_ref=ty, dst_ref=ry, send_sem=y_sem.at[0], recv_sem=y_sem.at[1],
            device_id={"head": pair}, device_id_type=MESH,
        )

    sides = (1 - y, y)
    stage1 = []
    direct = []
    for i, side in enumerate(sides):
        far = xo * 2 + side
        stage1.append((
            copy(0, i, p.at[far, top], r1p.at[i], nxt),
            copy(1, i, p.at[far, bottom], r1m.at[i], prv),
        ))
        direct.append((
            copy(2, i, p.at[xn * 2 + side, bottom], r2p.at[i, bottom], nxt),
            copy(3, i, p.at[xp * 2 + side, top], r2m.at[i, top], prv),
        ))
    for i in range(2):
        for c in stage1[i]:
            c.start()
        for c in direct[i]:
            c.start()
    stage2 = []
    for i, side in enumerate(sides):
        stage1[i][0].wait_recv()
        t2p[i] = p[xn * 2 + side, top] + r1p[i]
        a = copy(4, i, t2p.at[i], r2p.at[i, top], nxt)
        a.start()
        stage1[i][1].wait_recv()
        t2m[i] = p[xp * 2 + side, bottom] + r1m[i]
        b = copy(5, i, t2m.at[i], r2m.at[i, bottom], prv)
        b.start()
        stage2.append((a, b))
    for i, side in enumerate(sides):
        for c in direct[i] + stage2[i]:
            c.wait_recv()
        total = (
            p[x * 2 + side].astype(jnp.float32)
            + r2p[i].astype(jnp.float32)
            + r2m[i].astype(jnp.float32)
        )
        if i == 0:
            ty[...] = total.astype(BF)
            cross(0).start()
        else:
            cross(0).wait_recv()
            out[...] = (total + ry[...].astype(jnp.float32)).astype(BF)
    for i in range(2):
        for c in stage1[i] + direct[i] + stage2[i]:
            c.wait_send()
    cross(0).wait_send()


def mix(p):
    dma = pltpu.SemaphoreType.DMA
    width = LH * HD
    halfs = pltpu.VMEM((2, TOK // 2, width), BF)
    fulls = pltpu.VMEM((2, TOK, width), BF)
    one = pltpu.VMEM((TOK, width), BF)
    return pl.pallas_call(
        mix_kernel,
        out_shape=jax.ShapeDtypeStruct((TOK, width), BF),
        in_specs=[VMEM],
        out_specs=VMEM,
        scratch_shapes=[
            halfs, halfs, halfs, halfs, fulls, fulls, one, one, dma((6, 2)), dma((6, 2)), dma((2,)),
        ],
        compiler_params=pltpu.CompilerParams(
            collective_id=1, has_side_effects=True, vmem_limit_bytes=32 << 20
        ),
        name="mix_heads",
    )(p)


def body(query_rows, key_rows, value_rows, pattern, owners, out_weight):
    kv = gather(owners, key_rows, value_rows)
    return mix(attend(pattern, query_rows, kv, out_weight))


def solution(mesh):
    return jax.shard_map(
        body,
        mesh=mesh,
        in_specs=(
            P("seq", "head"),
            P("seq", "head"),
            P("seq", "head"),
            P("seq", None),
            P(),
            P("head", None),
        ),
        out_specs=P("seq", "head"),
        check_vma=False,
    )
```

time: 712 us -> 136 us (0.19)
  waiting for transfers between devices: 616 us -> 0 us
  Pallas kernels: 0 us -> 130 us
  starting transfers between devices: 29.6 us -> 0 us
  local copies, waits for them, and re-layouts: 27.4 us -> 5.67 us
  between operations: 20 us -> 0.04 us
  matrix products: 11.8 us -> 0 us
    psum x1 -> x0, waiting for transfers between devices: 520 us -> none  [broadcast(): return lax.psum(block, axis)]
    pallas_call x0 -> x3, Pallas kernels: none -> 130 us  [the longest x1 89.2 us: gather(): pl.pallas_call(gather_kernel, out_shape=jax.ShapeDtypeStruct((HK, PAD, HD...]
    unnamed x3 -> x0, waiting for transfers between devices: 95.9 us -> none
    ppermute x6 -> x0, starting transfers between devices: 29.6 us -> none  [from_behind(): return lax.ppermute(value, axis, pairs)]
    dot_general x19 -> x0, matrix products: 11.8 us -> none  [the longest x9 5.29 us: merge_block(): jnp.einsum('hqk,khd->hqd', weights.astype(jnp.bfloat16), values_three, pr...]
    another operation x5 -> x0, local copies, waits for them, and re-layouts: 8.34 us -> none
    slice x10 -> x0, local copies, waits for them, and re-layouts: 7.82 us -> none  [the longest x4 4.44 us: absorb(): stacked[1]]
  transfers between devices with their start and end apart: 8 -> 0, of which waited for: 2 -> 0; matrix products, arithmetic and copies ran while one was open for 4% -> 0% of each run, Pallas kernels for 0% -> 0%
where the time goes in v1:
time: 136 us
  Pallas kernels  130 us (96%)
  local copies, waits for them, and re-layouts  5.67 us (4%)
    pallas_call x1, Pallas kernels, gather(): pl.pallas_call(gather_kernel, out_shape=jax.ShapeDtypeStruct((HK, PAD, HD...  89.2 us
    pallas_call x1, Pallas kernels, mix(): pl.pallas_call(mix_kernel, out_shape=jax.ShapeDtypeStruct((TOK, width), B...  31.2 us
    pallas_call x1, Pallas kernels, attend(): pl.pallas_call(attend_kernel, out_shape=jax.ShapeDtypeStruct((2 * NX, TOK...  9.66 us
    unnamed x15, local copies, waits for them, and re-layouts  5.67 us

profile of v1, /device:TPU:1, one launch (start us, length us, event | category | flops | bytes accessed | tf_op | source)
XLA Modules:
  0.0 135.8 jit_solution(10038270529341203266)
XLA Ops:
  0.0 0.0 copy-start.1
  0.0 0.0 copy-start.2
  0.0 1.1 copy-done.2
  1.1 0.0 copy-start.3
  1.1 0.9 copy-done.3
  2.0 0.0 copy-start.5
  2.0 0.7 copy-done.5
  2.7 0.0 copy-start.4
  2.7 0.0 copy-start.6
  2.7 89.2 %gather_keys.1.kv = bf16[6,3328,128]{2,1,0:T(8,128)(2,1)S(1)} custom-call(s32[4]{0:T(128)S(1)} %copy-done.5, bf16[320,384]{1,0:T(8,128)(2,1)S(1)} %copy-done.2, bf16[320,384]{1,0:T(8,128)(2,1)S(1)} %copy-done.3), custom_call_target="tpu_custom_call" | custom-call | tf_op jit(solution)/shard_map/gather_keys/pallas_call | solution.py:324
  91.9 0.0 copy-start
  91.9 2.3 %copy-done = bf16[6,3328,128]{2,1,0:T(8,128)(2,1)} copy-done((bf16[6,3328,128]{2,1,0:T(8,128)(2,1)}, bf16[6,3328,128]{2,1,0:T(8,128)(2,1)S(1)}, u32[]{:S(2)}) %copy-start) | copy-done | bytes 5111832
  94.2 0.0 copy-done.1
  94.2 0.0 copy-done.4
  94.2 0.0 copy-done.6
  94.2 9.7 %attend.1.p = bf16[8,320,384]{2,1,0:T(8,128)(2,1)S(1)} custom-call(s32[1,6]{1,0:T(1,128)S(1)} %copy-done.6, bf16[320,384]{1,0:T(8,128)(2,1)S(1)} %copy-done.4, bf16[6,3328,128]{2,1,0:T(8,128)(2,1)} %copy-done, bf16[384,3072]{1,0:T(8,128)(2,1)S(1)} %copy-done.1), custom_call_target="tpu_custom_call" | custom-call | tf_op jit(solution)/shard_map/attend/pallas_call | solution.py:379
  103.9 31.2 %mix_heads.1 = bf16[320,384]{1,0:T(8,128)(2,1)S(1)} custom-call(bf16[8,320,384]{2,1,0:T(8,128)(2,1)S(1)} %attend.1.p), custom_call_target="tpu_custom_call" | custom-call | tf_op jit(solution)/shard_map/mix_heads/pallas_call | solution.py:474
  135.1 0.7 copy.8
Async XLA Ops:
  0.0 94.2 %copy-start.1 = (bf16[384,3072]{1,0:T(8,128)(2,1)S(1)}, bf16[384,3072]{1,0:T(8,128)(2,1)}, u32[]{:S(2)}) copy-start(bf16[384,3072]{1,0:T(8,128)(2,1)} %w_ref.1) | copy-start | bytes 7077892
  0.0 1.1 copy-start.2
  1.1 0.9 copy-start.3
  2.0 0.7 copy-start.5
  2.7 91.5 %copy-start.4 = (bf16[320,384]{1,0:T(8,128)(2,1)S(1)}, bf16[320,384]{1,0:T(8,128)(2,1)}, u32[]{:S(2)}) copy-start(bf16[320,384]{1,0:T(8,128)(2,1)} %q_ref.1) | copy-start | bytes 737284
  2.7 91.5 %copy-start.6 = (s32[1,6]{1,0:T(1,128)S(1)}, s32[1,6]{1,0:T(1,128)}, u32[]{:S(2)}) copy-start(s32[1,6]{1,0:T(1,128)} %pattern_ref.1) | copy-start | bytes 76
  91.9 2.3 %copy-start = (bf16[6,3328,128]{2,1,0:T(8,128)(2,1)}, bf16[6,3328,128]{2,1,0:T(8,128)(2,1)S(1)}, u32[]{:S(2)}) copy-start(bf16[6,3328,128]{2,1,0:T(8,128)(2,1)S(1)} %gather_keys.1.kv) | copy-start | bytes 15335428

commit v2 on v1

v2 whole, which is shorter than its diff:
```python
import functools

import jax
import jax.numpy as jnp
from jax import lax
from jax.experimental import pallas as pl
from jax.experimental.pallas import tpu as pltpu
from jax.sharding import PartitionSpec as P

MESH = pl.DeviceIdType.MESH
HD = 128
LH = 3
TOK = 320
REF = 256
REACH = 3
NZ = 8
NY = 4
NX = 4
HK = 2 * LH
PIECE = REF // NZ
OWN = 4 * REF
HALO = OWN + TOK
KEYS = HALO + 2 * REACH * TOK
PAD = -(-KEYS // 256) * 256
NEG = -1e30
VMEM = pl.BlockSpec(memory_space=pltpu.VMEM)
SMEM = pl.BlockSpec(memory_space=pltpu.SMEM)
BF = jnp.bfloat16


def gather_kernel(
    owners_ref, k_ref, v_ref, kv, mine, msend, mrecv, ps, pr, ss, sr, ysend, yr,
    hs_sem, hr_sem, m_sem, p_sem, s_sem, x_sem, y_sem, ys_sem, a_sem, b_sem, f_sem,
):
    s = lax.axis_index("seq")
    n = 2 * NZ * NY
    core = lax.rem(s, 2)
    z = lax.rem(s // 2, NZ)
    y = s // (2 * NZ)
    step = 1 - 2 * core
    pz = jnp.where(core == 0, z, NZ - 1 - z)
    py = jnp.where(core == 0, y, NY - 1 - y)
    right = lax.rem(s + 2, n)
    left = lax.rem(s - 2 + n, n)
    partner = s + step
    extra = lax.rem(s - step + n, n)

    def at(yy, zz):
        zz = lax.rem(zz + NZ, NZ)
        yy = lax.rem(yy + NY, NY)
        zz = jnp.where(core == 0, zz, NZ - 1 - zz)
        yy = jnp.where(core == 0, yy, NY - 1 - yy)
        return (yy * NZ + zz) * 2 + core

    ahead = at(py, pz + 1)
    behind = at(py, pz - 1)

    barrier = pltpu.get_barrier_semaphore()
    peers = [partner, right, left, extra]
    peers += [at(py, pz + d) for d in range(1, NZ)]
    peers += [at(py + d, pz) for d in range(1, NY)]
    for peer in peers:
        pl.semaphore_signal(barrier, inc=1, device_id={"seq": peer}, device_id_type=MESH)

    for h in range(LH):
        cols = slice(h * HD, (h + 1) * HD)
        kv[2 * h, OWN:HALO, :] = k_ref[:, cols]
        kv[2 * h + 1, OWN:HALO, :] = v_ref[:, cols]
    if PAD > KEYS:
        kv[:, KEYS:PAD, :] = jnp.zeros((HK, PAD - KEYS, HD), BF)

    low = jnp.int32(n)
    high = jnp.int32(-1)
    for i in range(4):
        o = owners_ref[i]
        low = jnp.minimum(low, jnp.where(o == 0, n, o))
        high = jnp.maximum(high, jnp.where(o == n - 1, -1, o))
    wanted = jnp.where(core == 0, low, high)
    given = jnp.where(core == 0, high, low)
    keep = jnp.where(wanted == s, 1.0, 0.0).astype(BF)
    give = jnp.where(given == s, 1.0, 0.0).astype(BF)
    for hk in range(HK):
        block = kv[hk, OWN : OWN + REF, :]
        mine[hk] = block * keep
        msend[hk] = block * give

    pl.semaphore_wait(barrier, len(peers))

    def remote(src, dst, send, recv, peer):
        return pltpu.make_async_remote_copy(
            src_ref=src, dst_ref=dst, send_sem=send, recv_sem=recv,
            device_id={"seq": peer}, device_id_type=MESH,
        )

    def planes(ref, g):
        return ref.at[2 * g : 2 * g + 2]

    def swap(g):
        return remote(planes(msend, g), planes(mrecv, g), m_sem.at[0, g], m_sem.at[1, g], partner)

    def p_copy(j, g):
        return remote(ps.at[j, g], pr.at[j, g], p_sem.at[0, j, g], p_sem.at[1, j, g], ahead)

    def s_copy(j, g):
        return remote(ss.at[j, g], sr.at[j, g], s_sem.at[0, j, g], s_sem.at[1, j, g], behind)

    base = core * 2 * REF

    def piece(g, q, first, count):
        start = base + lax.rem(q + NZ, NZ) * 2 * PIECE + first
        return kv.at[2 * g : 2 * g + 2, pl.ds(pl.multiple_of(start, PIECE), count)]

    def mine_rows(g, q):
        start = lax.rem(q + NZ, NZ) * PIECE
        return mine[2 * g : 2 * g + 2, pl.ds(pl.multiple_of(start, PIECE), PIECE), :]

    def fixed_copy(q, g):
        return remote(
            kv.at[2 * g : 2 * g + 2, OWN + q * PIECE : OWN + (q + 1) * PIECE],
            piece(g, q, PIECE, PIECE), x_sem.at[0, q, g], x_sem.at[1, 0, g], at(0, q),
        )

    def y_copy(d, g):
        return remote(planes(ysend, g), yr.at[d - 1, g], y_sem.at[0, d, g], y_sem.at[1, d, g], at(py + d, pz))

    def y_fixed(d, g):
        part = piece(g, pz, PIECE, PIECE)
        return remote(part, part, ys_sem.at[0, d, g], ys_sem.at[1, 0, g], at(py + d, pz))

    def around(j, g):
        part = piece(g, pz - j, 0, 2 * PIECE)
        return remote(part, part, a_sem.at[0, j, g], a_sem.at[1, j, g], ahead)

    def around_arrived(j, g):
        part = piece(g, pz - j - 1, 0, 2 * PIECE)
        remote(part, part, a_sem.at[0, j, g], a_sem.at[1, j, g], ahead).wait_recv()

    def back(j, g):
        part = piece(g, pz + j, 0, 2 * PIECE)
        return remote(part, part, b_sem.at[0, j, g], b_sem.at[1, j, g], behind)

    def back_arrived(j, g):
        part = piece(g, pz + j + 1, 0, 2 * PIECE)
        remote(part, part, b_sem.at[0, j, g], b_sem.at[1, j, g], behind).wait_recv()

    def share(g):
        part = kv.at[2 * g : 2 * g + 2, pl.ds(pl.multiple_of(base, PIECE), 2 * REF)]
        return remote(part, part, f_sem.at[0, g], f_sem.at[1, g], partner)

    def shared(g):
        part = kv.at[2 * g : 2 * g + 2, pl.ds(pl.multiple_of(2 * REF - base, PIECE), 2 * REF)]
        remote(part, part, f_sem.at[0, g], f_sem.at[1, g], partner).wait_recv()

    def halo_rows(g, col):
        return kv.at[2 * g : 2 * g + 2, pl.ds(pl.multiple_of(HALO + col * TOK, 16), TOK)]

    def halo_copy(kind, src, g, col, peer):
        return remote(src, halo_rows(g, col), hs_sem.at[kind, g], hr_sem.at[col, g], peer)

    def own_rows(g):
        return kv.at[2 * g : 2 * g + 2, OWN:HALO]

    def halo_sends(g):
        return (
            halo_copy(0, own_rows(g), g, 1, right),
            halo_copy(1, own_rows(g), g, 4, left),
            halo_copy(2, own_rows(g), g, 2 + core, partner),
        )

    def forwards(g):
        return (
            halo_copy(3, halo_rows(g, 1), g, 2 * core, partner),
            halo_copy(4, halo_rows(g, 4), g, 3 + 2 * core, partner),
            halo_copy(5, halo_rows(g, 4 - 3 * core), g, 5 - 5 * core, extra),
        )

    def halo_wait(g, col):
        halo_copy(0, own_rows(g), g, col, right).wait_recv()

    def halo_start(g):
        for copy in halo_sends(g):
            copy.start()

    def halo_forward(g):
        halo_wait(g, 1)
        halo_wait(g, 4)
        for copy in forwards(g):
            copy.start()

    source = (pz == 0) & (py == 0)
    heads = range(LH)
    for g in heads:
        swap(g).start()

    @pl.when(source)
    def _():
        for g in heads:
            for q in range(1, NZ):
                fixed_copy(q, g).start()
            part = kv[2 * g : 2 * g + 2, OWN : OWN + PIECE, :]
            piece(g, 0, PIECE, PIECE)[...] = part

    halo_start(0)
    far, near = NZ // 2, NZ // 2 - 1
    for j in range(far):
        for g in heads:
            if j == 0:
                swap(g).wait_recv()
                mine[2 * g : 2 * g + 2] = mine[2 * g : 2 * g + 2] + mrecv[2 * g : 2 * g + 2]
                ps[0, g] = mine_rows(g, pz + far)
                p_copy(0, g).start()
                if near > 0:
                    ss[0, g] = mine_rows(g, pz - near)
                    s_copy(0, g).start()
            else:
                p_copy(j - 1, g).wait_recv()
                ps[j, g] = mine_rows(g, pz + far - j) + pr[j - 1, g]
                p_copy(j, g).start()
                if j < near:
                    s_copy(j - 1, g).wait_recv()
                    ss[j, g] = mine_rows(g, pz - near + j) + sr[j - 1, g]
                    s_copy(j, g).start()
        if j == 1:
            halo_start(1)
        if j == 2:
            halo_start(2)
    for g in heads:
        total = mine_rows(g, pz)
        if near > 0:
            s_copy(near - 1, g).wait_recv()
            total = total + sr[near - 1, g]
        p_copy(far - 1, g).wait_recv()
        ysend[2 * g : 2 * g + 2] = total + pr[far - 1, g]
        for d in range(1, NY):
            y_copy(d, g).start()

        @pl.when(py == 0)
        def _():
            @pl.when(pz > 0)
            def _():
                part = piece(g, pz, PIECE, PIECE)
                remote(part, part, x_sem.at[0, 0, g], x_sem.at[1, 0, g], ahead).wait_recv()

            for d in range(1, NY):
                y_fixed(d, g).start()

    halo_forward(0)
    for g in heads:
        total = ysend[2 * g : 2 * g + 2]
        for d in range(1, NY):
            y_copy(d, g).wait_recv()
            total = total + yr[d - 1, g]
        piece(g, pz, 0, PIECE)[...] = total

        @pl.when(py > 0)
        def _():
            part = piece(g, pz, PIECE, PIECE)
            remote(part, part, ys_sem.at[0, 0, g], ys_sem.at[1, 0, g], ahead).wait_recv()

        around(0, g).start()
        if near > 0:
            back(0, g).start()
    for j in range(1, far):
        for g in heads:
            around_arrived(j - 1, g)
            around(j, g).start()
            if j < near:
                back_arrived(j - 1, g)
                back(j, g).start()
        if j < 3:
            halo_forward(j)
    if far < 3:
        for g in range(max(far, 1), 3):
            halo_forward(g)
    for g in heads:
        around_arrived(far - 1, g)
        if near > 0:
            back_arrived(near - 1, g)
        share(g).start()
    for g in heads:
        shared(g)
        for col in (0, 2, 3, 5):
            halo_wait(g, col)

    for g in heads:
        swap(g).wait_send()
        share(g).wait_send()
        for j in range(far):
            p_copy(j, g).wait_send()
            around(j, g).wait_send()
        for j in range(near):
            s_copy(j, g).wait_send()
            back(j, g).wait_send()
        for d in range(1, NY):
            y_copy(d, g).wait_send()
        for copy in halo_sends(g) + forwards(g):
            copy.wait_send()

        @pl.when(py == 0)
        def _():
            for d in range(1, NY):
                y_fixed(d, g).wait_send()

        @pl.when(source)
        def _():
            for q in range(1, NZ):
                fixed_copy(q, g).wait_send()


def gather(owners, k, v):
    dma = pltpu.SemaphoreType.DMA
    whole = pltpu.VMEM((HK, REF, HD), BF)
    hop = pltpu.VMEM((NZ // 2, LH, 2, PIECE, HD), BF)
    return pl.pallas_call(
        gather_kernel,
        out_shape=jax.ShapeDtypeStruct((HK, PAD, HD), BF),
        in_specs=[SMEM, VMEM, VMEM],
        out_specs=VMEM,
        scratch_shapes=[
            whole, whole, whole, hop, hop, hop, hop,
            pltpu.VMEM((HK, PIECE, HD), BF), pltpu.VMEM((NY - 1, LH, 2, PIECE, HD), BF),
            dma((6, LH)), dma((6, LH)), dma((2, LH)), dma((2, NZ // 2, LH)), dma((2, NZ // 2, LH)),
            dma((2, NZ, LH)), dma((2, NY, LH)), dma((2, NY, LH)),
            dma((2, NZ // 2, LH)), dma((2, NZ // 2, LH)), dma((2, LH)),
        ],
        compiler_params=pltpu.CompilerParams(
            collective_id=0, has_side_effects=True, vmem_limit_bytes=40 << 20
        ),
        name="gather_keys",
    )(owners, k, v)


def attend_kernel(pattern_ref, q_ref, kv, w_ref, out, scores, att):
    position = lax.broadcasted_iota(jnp.int32, (1, PAD), 1)
    bias = jnp.where(position >= KEYS, NEG, 0.0)
    for col in range(2 * REACH):
        low = HALO + col * TOK
        closed = jnp.where(pattern_ref[0, col] != 0, 0.0, NEG)
        bias = bias + jnp.where((position >= low) & (position < low + TOK), closed, 0.0)
    scale = HD ** -0.5
    for h in range(LH):
        q = q_ref[:, h * HD : (h + 1) * HD]
        peak = jnp.full((TOK, HD), NEG, jnp.float32)
        for t in range(PAD // 256):
            keys = kv[2 * h, t * 256 : (t + 1) * 256, :]
            sc = lax.dot_general(
                q, keys, (((1,), (1,)), ((), ())), preferred_element_type=jnp.float32
            )
            sc = sc * scale + bias[:, t * 256 : (t + 1) * 256]
            scores[:, t * 256 : (t + 1) * 256] = sc
            peak = jnp.maximum(peak, jnp.maximum(sc[:, :128], sc[:, 128:]))
        top = jnp.max(peak, axis=1, keepdims=True)
        total = jnp.zeros((TOK, HD), jnp.float32)
        acc = jnp.zeros((TOK, HD), jnp.float32)
        for t in range(PAD // 256):
            w = jnp.exp(scores[:, t * 256 : (t + 1) * 256] - top)
            total = total + (w[:, :128] + w[:, 128:])
            acc = acc + jnp.dot(
                w.astype(BF), kv[2 * h + 1, t * 256 : (t + 1) * 256, :],
                preferred_element_type=jnp.float32,
            )
        total = jnp.sum(total, axis=1, keepdims=True)
        att[:, h * HD : (h + 1) * HD] = (acc / total).astype(BF)
    width = LH * HD
    for b in range(2 * NX):
        out[b] = jnp.dot(
            att[...], w_ref[:, b * width : (b + 1) * width], preferred_element_type=jnp.float32
        ).astype(BF)


def attend(pattern, q, kv, w):
    return pl.pallas_call(
        attend_kernel,
        out_shape=jax.ShapeDtypeStruct((2 * NX, TOK, LH * HD), BF),
        in_specs=[SMEM, VMEM, VMEM, VMEM],
        out_specs=VMEM,
        scratch_shapes=[pltpu.VMEM((TOK, PAD), jnp.float32), pltpu.VMEM((TOK, LH * HD), BF)],
        compiler_params=pltpu.CompilerParams(vmem_limit_bytes=48 << 20),
        name="attend",
    )(pattern, q, kv, w)


def mix_kernel(p, out, r1p, r1m, t2p, t2m, r2p, r2m, ty, ry, s_sem, r_sem, y_sem):
    h = lax.axis_index("head")
    x = h // 2
    y = lax.rem(h, 2)
    xn = lax.rem(x + 1, NX)
    xp = lax.rem(x + NX - 1, NX)
    xo = lax.rem(x + 2, NX)
    nxt = xn * 2 + y
    prv = xp * 2 + y
    pair = x * 2 + 1 - y
    barrier = pltpu.get_barrier_semaphore()
    for peer in (nxt, prv, pair):
        pl.semaphore_signal(barrier, inc=1, device_id={"head": peer}, device_id_type=MESH)
    pl.semaphore_wait(barrier, 3)
    half = TOK // 2
    top, bottom = slice(0, half), slice(half, TOK)

    def copy(kind, i, src, dst, peer):
        return pltpu.make_async_remote_copy(
            src_ref=src, dst_ref=dst, send_sem=s_sem.at[kind, i], recv_sem=r_sem.at[kind, i],
            device_id={"head": peer}, device_id_type=MESH,
        )

    def cross(i):
        return pltpu.make_async_remote_copy(
            src_ref=ty, dst_ref=ry, send_sem=y_sem.at[0], recv_sem=y_sem.at[1],
            device_id={"head": pair}, device_id_type=MESH,
        )

    sides = (1 - y, y)
    stage1 = []
    direct = []
    for i, side in enumerate(sides):
        far = xo * 2 + side
        stage1.append((
            copy(0, i, p.at[far, top], r1p.at[i], nxt),
            copy(1, i, p.at[far, bottom], r1m.at[i], prv),
        ))
        direct.append((
            copy(2, i, p.at[xn * 2 + side, bottom], r2p.at[i, bottom], nxt),
            copy(3, i, p.at[xp * 2 + side, top], r2m.at[i, top], prv),
        ))
    for i in range(2):
        for c in stage1[i]:
            c.start()
        for c in direct[i]:
            c.start()
    stage2 = []
    for i, side in enumerate(sides):
        stage1[i][0].wait_recv()
        t2p[i] = p[xn * 2 + side, top] + r1p[i]
        a = copy(4, i, t2p.at[i], r2p.at[i, top], nxt)
        a.start()
        stage1[i][1].wait_recv()
        t2m[i] = p[xp * 2 + side, bottom] + r1m[i]
        b = copy(5, i, t2m.at[i], r2m.at[i, bottom], prv)
        b.start()
        stage2.append((a, b))
    for i, side in enumerate(sides):
        for c in direct[i] + stage2[i]:
            c.wait_recv()
        total = (
            p[x * 2 + side].astype(jnp.float32)
            + r2p[i].astype(jnp.float32)
            + r2m[i].astype(jnp.float32)
        )
        if i == 0:
            ty[...] = total.astype(BF)
            cross(0).start()
        else:
            cross(0).wait_recv()
            out[...] = (total + ry[...].astype(jnp.float32)).astype(BF)
    for i in range(2):
        for c in stage1[i] + direct[i] + stage2[i]:
            c.wait_send()
    cross(0).wait_send()


def mix(p):
    dma = pltpu.SemaphoreType.DMA
    width = LH * HD
    halfs = pltpu.VMEM((2, TOK // 2, width), BF)
    fulls = pltpu.VMEM((2, TOK, width), BF)
    one = pltpu.VMEM((TOK, width), BF)
    return pl.pallas_call(
        mix_kernel,
        out_shape=jax.ShapeDtypeStruct((TOK, width), BF),
        in_specs=[VMEM],
        out_specs=VMEM,
        scratch_shapes=[
            halfs, halfs, halfs, halfs, fulls, fulls, one, one, dma((6, 2)), dma((6, 2)), dma((2,)),
        ],
        compiler_params=pltpu.CompilerParams(
            collective_id=1, has_side_effects=True, vmem_limit_bytes=32 << 20
        ),
        name="mix_heads",
    )(p)


def body(query_rows, key_rows, value_rows, pattern, owners, out_weight):
    kv = gather(owners, key_rows, value_rows)
    return mix(attend(pattern, query_rows, kv, out_weight))


def solution(mesh):
    return jax.shard_map(
        body,
        mesh=mesh,
        in_specs=(
            P("seq", "head"),
            P("seq", "head"),
            P("seq", "head"),
            P("seq", None),
            P(),
            P("head", None),
        ),
        out_specs=P("seq", "head"),
        check_vma=False,
    )
```

time: 136 us -> 112 us (0.82)
  the two profiles are of different devices: /device:TPU:1 before, /device:TPU:49 now
where the time goes in v2:
time: 112 us
  Pallas kernels  106 us (95%)
  local copies, waits for them, and re-layouts  5.67 us (5%)
    pallas_call x1, Pallas kernels, gather(): pl.pallas_call(gather_kernel, out_shape=jax.ShapeDtypeStruct((HK, PAD, HD...  65.4 us
    pallas_call x1, Pallas kernels, mix(): pl.pallas_call(mix_kernel, out_shape=jax.ShapeDtypeStruct((TOK, width), B...  30.8 us
    pallas_call x1, Pallas kernels, attend(): pl.pallas_call(attend_kernel, out_shape=jax.ShapeDtypeStruct((2 * NX, TOK...  9.66 us
    unnamed x15, local copies, waits for them, and re-layouts  5.67 us

profile of v2, /device:TPU:49, one launch (start us, length us, event | category | flops | bytes accessed | tf_op | source)
XLA Modules:
  0.0 111.6 jit_solution(17547658122373393410)
XLA Ops:
  0.0 0.0 copy-start.1
  0.0 0.0 copy-start.2
  0.0 1.1 copy-done.2
  1.1 0.0 copy-start.3
  1.1 0.9 copy-done.3
  2.0 0.0 copy-start.5
  2.0 0.7 copy-done.5
  2.7 0.0 copy-start.4
  2.7 0.0 copy-start.6
  2.7 65.4 %gather_keys.1.kv = bf16[6,3328,128]{2,1,0:T(8,128)(2,1)S(1)} custom-call(s32[4]{0:T(128)S(1)} %copy-done.5, bf16[320,384]{1,0:T(8,128)(2,1)S(1)} %copy-done.2, bf16[320,384]{1,0:T(8,128)(2,1)S(1)} %copy-done.3), custom_call_target="tpu_custom_call" | custom-call | tf_op jit(solution)/shard_map/gather_keys/pallas_call | solution.py:314
  68.1 0.0 copy-start
  68.2 2.3 %copy-done = bf16[6,3328,128]{2,1,0:T(8,128)(2,1)} copy-done((bf16[6,3328,128]{2,1,0:T(8,128)(2,1)}, bf16[6,3328,128]{2,1,0:T(8,128)(2,1)S(1)}, u32[]{:S(2)}) %copy-start) | copy-done | bytes 5111832
  70.4 0.0 copy-done.1
  70.4 0.0 copy-done.4
  70.4 0.0 copy-done.6
  70.4 9.7 %attend.1.p = bf16[8,320,384]{2,1,0:T(8,128)(2,1)S(1)} custom-call(s32[1,6]{1,0:T(1,128)S(1)} %copy-done.6, bf16[320,384]{1,0:T(8,128)(2,1)S(1)} %copy-done.4, bf16[6,3328,128]{2,1,0:T(8,128)(2,1)} %copy-done, bf16[384,3072]{1,0:T(8,128)(2,1)S(1)} %copy-done.1), custom_call_target="tpu_custom_call" | custom-call | tf_op jit(solution)/shard_map/attend/pallas_call | solution.py:372
  80.1 30.8 %mix_heads.1 = bf16[320,384]{1,0:T(8,128)(2,1)S(1)} custom-call(bf16[8,320,384]{2,1,0:T(8,128)(2,1)S(1)} %attend.1.p), custom_call_target="tpu_custom_call" | custom-call | tf_op jit(solution)/shard_map/mix_heads/pallas_call | solution.py:467
  111.0 0.7 copy.8
Async XLA Ops:
  0.0 70.4 %copy-start.1 = (bf16[384,3072]{1,0:T(8,128)(2,1)S(1)}, bf16[384,3072]{1,0:T(8,128)(2,1)}, u32[]{:S(2)}) copy-start(bf16[384,3072]{1,0:T(8,128)(2,1)} %w_ref.1) | copy-start | bytes 7077892
  0.0 1.1 copy-start.2
  1.1 0.9 copy-start.3
  2.0 0.7 copy-start.5
  2.7 67.7 %copy-start.4 = (bf16[320,384]{1,0:T(8,128)(2,1)S(1)}, bf16[320,384]{1,0:T(8,128)(2,1)}, u32[]{:S(2)}) copy-start(bf16[320,384]{1,0:T(8,128)(2,1)} %q_ref.1) | copy-start | bytes 737284
  2.7 67.7 %copy-start.6 = (s32[1,6]{1,0:T(1,128)S(1)}, s32[1,6]{1,0:T(1,128)}, u32[]{:S(2)}) copy-start(s32[1,6]{1,0:T(1,128)} %pattern_ref.1) | copy-start | bytes 76
  68.1 2.3 %copy-start = (bf16[6,3328,128]{2,1,0:T(8,128)(2,1)}, bf16[6,3328,128]{2,1,0:T(8,128)(2,1)S(1)}, u32[]{:S(2)}) copy-start(bf16[6,3328,128]{2,1,0:T(8,128)(2,1)S(1)} %gather_keys.1.kv) | copy-start | bytes 15335428

commit v3 on v2

--- a/solution.py
+++ b/solution.py
@@ -23,16 +23,31 @@
 KEYS = HALO + 2 * REACH * TOK
 PAD = -(-KEYS // 256) * 256
 NEG = -1e30
+TILE = 256
+PARTS = 2
 VMEM = pl.BlockSpec(memory_space=pltpu.VMEM)
 SMEM = pl.BlockSpec(memory_space=pltpu.SMEM)
 BF = jnp.bfloat16
 
 
-def gather_kernel(
-    owners_ref, k_ref, v_ref, kv, mine, msend, mrecv, ps, pr, ss, sr, ysend, yr,
+def layer_kernel(
+    owners_ref, pattern_ref, q_hbm, k_hbm, v_hbm, w_hbm, out,
+    kv, qb, wb, mine, msend, mrecv, ps, pr, ss, sr, ysend, yr,
+    scores, att, acc1, top1, total1, p, r1p, r1m, t2p, t2m, r2p, r2m, ty, ry,
     hs_sem, hr_sem, m_sem, p_sem, s_sem, x_sem, y_sem, ys_sem, a_sem, b_sem, f_sem,
+    in_sem, w_sem, q_sem, mix_s, mix_r, c_sem,
 ):
     s = lax.axis_index("seq")
+    head = lax.axis_index("head")
+    x = head // 2
+    side = lax.rem(head, 2)
+    xn = lax.rem(x + 1, NX)
+    xp = lax.rem(x + NX - 1, NX)
+    xo = lax.rem(x + 2, NX)
+    nxt = xn * 2 + side
+    prv = xp * 2 + side
+    pair = x * 2 + 1 - side
+    width = LH * HD
     n = 2 * NZ * NY
     core = lax.rem(s, 2)
     z = lax.rem(s // 2, NZ)
@@ -55,17 +70,28 @@
     ahead = at(py, pz + 1)
     behind = at(py, pz - 1)
 
+    loads = []
+    for h in range(LH):
+        for i, ref in enumerate((k_hbm, v_hbm)):
+            loads.append(pltpu.make_async_copy(
+                ref.at[:, h * HD : (h + 1) * HD], kv.at[2 * h + i, OWN:HALO], in_sem.at[2 * h + i]
+            ))
+            loads[-1].start()
+
     barrier = pltpu.get_barrier_semaphore()
     peers = [partner, right, left, extra]
     peers += [at(py, pz + d) for d in range(1, NZ)]
     peers += [at(py + d, pz) for d in range(1, NY)]
     for peer in peers:
         pl.semaphore_signal(barrier, inc=1, device_id={"seq": peer}, device_id_type=MESH)
-
-    for h in range(LH):
-        cols = slice(h * HD, (h + 1) * HD)
-        kv[2 * h, OWN:HALO, :] = k_ref[:, cols]
-        kv[2 * h + 1, OWN:HALO, :] = v_ref[:, cols]
+    for peer in (nxt, prv, pair):
+        pl.semaphore_signal(barrier, inc=1, device_id={"head": peer}, device_id_type=MESH)
+
+    query_load = pltpu.make_async_copy(q_hbm, qb, q_sem)
+    weight_loads = [
+        pltpu.make_async_copy(w_hbm.at[:, b * width : (b + 1) * width], wb.at[b], w_sem.at[b])
+        for b in range(2 * NX)
+    ]
     if PAD > KEYS:
         kv[:, KEYS:PAD, :] = jnp.zeros((HK, PAD - KEYS, HD), BF)
 
@@ -80,11 +106,12 @@
     keep = jnp.where(wanted == s, 1.0, 0.0).astype(BF)
     give = jnp.where(given == s, 1.0, 0.0).astype(BF)
     for hk in range(HK):
+        loads[hk].wait()
         block = kv[hk, OWN : OWN + REF, :]
         mine[hk] = block * keep
         msend[hk] = block * give
 
-    pl.semaphore_wait(barrier, len(peers))
+    pl.semaphore_wait(barrier, len(peers) + 3)
 
     def remote(src, dst, send, recv, peer):
         return pltpu.make_async_remote_copy(
@@ -186,6 +213,56 @@
         halo_wait(g, 4)
         for copy in forwards(g):
             copy.start()
+
+    position = lax.broadcasted_iota(jnp.int32, (1, PAD - OWN), 1) + OWN
+    bias = jnp.where(position >= KEYS, NEG, 0.0)
+    for col in range(2 * REACH):
+        edge = HALO + col * TOK
+        closed = jnp.where(pattern_ref[0, col] != 0, 0.0, NEG)
+        bias = bias + jnp.where((position >= edge) & (position < edge + TOK), closed, 0.0)
+    scale = HD ** -0.5
+
+    def segment(h, first, last):
+        q = qb[:, h * HD : (h + 1) * HD]
+        peak = jnp.full((TOK, HD), NEG, jnp.float32)
+        tiles = range(first, last, TILE)
+        for row in tiles:
+            sc = lax.dot_general(
+                q, kv[2 * h, row : row + TILE, :], (((1,), (1,)), ((), ())),
+                preferred_element_type=jnp.float32,
+            )
+            sc = sc * scale
+            if row >= OWN:
+                sc = sc + bias[:, row - OWN : row - OWN + TILE]
+            scores[:, row - first : row - first + TILE] = sc
+            peak = jnp.maximum(peak, jnp.maximum(sc[:, :HD], sc[:, HD:]))
+        top = jnp.max(peak, axis=1, keepdims=True)
+        total = jnp.zeros((TOK, HD), jnp.float32)
+        acc = jnp.zeros((TOK, HD), jnp.float32)
+        for row in tiles:
+            w = jnp.exp(scores[:, row - first : row - first + TILE] - top)
+            total = total + (w[:, :HD] + w[:, HD:])
+            acc = acc + jnp.dot(
+                w.astype(BF), kv[2 * h + 1, row : row + TILE, :], preferred_element_type=jnp.float32
+            )
+        return top, jnp.sum(total, axis=1, keepdims=True), acc
+
+    def near_part(h):
+        for col in range(2 * REACH):
+            if col not in (1, 4):
+                halo_wait(h, col)
+        top, total, acc = segment(h, OWN, PAD)
+        top1[h] = top
+        total1[h] = total
+        acc1[h] = acc
+
+    def far_part(h):
+        top, total, acc = segment(h, 0, OWN)
+        best = jnp.maximum(top, top1[h])
+        new = jnp.exp(top - best)
+        old = jnp.exp(top1[h] - best)
+        whole = total * new + total1[h] * old
+        att[:, h * HD : (h + 1) * HD] = ((acc * new + acc1[h] * old) / whole).astype(BF)
 
     source = (pz == 0) & (py == 0)
     heads = range(LH)
@@ -201,6 +278,9 @@
             piece(g, 0, PIECE, PIECE)[...] = part
 
     halo_start(0)
+    query_load.start()
+    for load in weight_loads:
+        load.start()
     far, near = NZ // 2, NZ // 2 - 1
     for j in range(far):
         for g in heads:
@@ -224,6 +304,14 @@
             halo_start(1)
         if j == 2:
             halo_start(2)
+            halo_forward(0)
+        if j == 3:
+            halo_forward(1)
+    if far <= 2:
+        halo_start(2)
+        halo_forward(0)
+    if far <= 3:
+        halo_forward(1)
     for g in heads:
         total = mine_rows(g, pz)
         if near > 0:
@@ -244,7 +332,7 @@
             for d in range(1, NY):
                 y_fixed(d, g).start()
 
-    halo_forward(0)
+    halo_forward(2)
     for g in heads:
         total = ysend[2 * g : 2 * g + 2]
         for d in range(1, NY):
@@ -260,6 +348,7 @@
         around(0, g).start()
         if near > 0:
             back(0, g).start()
+    query_load.wait()
     for j in range(1, far):
         for g in heads:
             around_arrived(j - 1, g)
@@ -267,11 +356,9 @@
             if j < near:
                 back_arrived(j - 1, g)
                 back(j, g).start()
-        if j < 3:
-            halo_forward(j)
-    if far < 3:
-        for g in range(max(far, 1), 3):
-            halo_forward(g)
+        near_part(j - 1)
+    for h in range(far - 1, LH):
+        near_part(h)
     for g in heads:
         around_arrived(far - 1, g)
         if near > 0:
@@ -279,8 +366,93 @@
         share(g).start()
     for g in heads:
         shared(g)
-        for col in (0, 2, 3, 5):
-            halo_wait(g, col)
+        far_part(g)
+
+    for load in weight_loads:
+        load.wait()
+
+    def project(b):
+        p[b] = jnp.dot(att[...], wb[b], preferred_element_type=jnp.float32).astype(BF)
+
+    def head_copy(kind, i, src, dst, peer):
+        return pltpu.make_async_remote_copy(
+            src_ref=src, dst_ref=dst, send_sem=mix_s.at[kind, i], recv_sem=mix_r.at[kind, i],
+            device_id={"head": peer}, device_id_type=MESH,
+        )
+
+    def cross(c):
+        return pltpu.make_async_remote_copy(
+            src_ref=ty.at[c], dst_ref=ry.at[c], send_sem=c_sem.at[0, c], recv_sem=c_sem.at[1, c],
+            device_id={"head": pair}, device_id_type=MESH,
+        )
+
+    part = TOK // PARTS
+    half = part // 2
+    items = [(which, c) for which in (1 - side, side) for c in range(PARTS)]
+    rows = [(slice(c * part, c * part + half), slice(c * part + half, (c + 1) * part)) for c in range(PARTS)]
+    first, direct, second = [], [], []
+    for i, (which, c) in enumerate(items):
+        upper, lower = rows[c]
+        first.append((
+            head_copy(0, i, p.at[xo * 2 + which, upper], r1p.at[i], nxt),
+            head_copy(1, i, p.at[xo * 2 + which, lower], r1m.at[i], prv),
+        ))
+        direct.append((
+            head_copy(2, i, p.at[xn * 2 + which, lower], r2p.at[i, half:], nxt),
+            head_copy(3, i, p.at[xp * 2 + which, upper], r2m.at[i, :half], prv),
+        ))
+        second.append((
+            head_copy(4, i, t2p.at[i], r2p.at[i, :half], nxt),
+            head_copy(5, i, t2m.at[i], r2m.at[i, half:], prv),
+        ))
+
+    def pass_on(i):
+        which, c = items[i]
+        upper, lower = rows[c]
+        first[i][0].wait_recv()
+        t2p[i] = p[xn * 2 + which, upper] + r1p[i]
+        second[i][0].start()
+        first[i][1].wait_recv()
+        t2m[i] = p[xp * 2 + which, lower] + r1m[i]
+        second[i][1].start()
+
+    def collect(i):
+        which, c = items[i]
+        for copy in direct[i] + second[i]:
+            copy.wait_recv()
+        return (
+            p[x * 2 + which, c * part : (c + 1) * part].astype(jnp.float32)
+            + r2p[i].astype(jnp.float32)
+            + r2m[i].astype(jnp.float32)
+        )
+
+    for phase in range(2):
+        which = items[phase * PARTS][0]
+        mineq = range(phase * PARTS, (phase + 1) * PARTS)
+        project(xo * 2 + which)
+        for i in mineq:
+            for copy in first[i]:
+                copy.start()
+        project(xn * 2 + which)
+        project(xp * 2 + which)
+        for i in mineq:
+            for copy in direct[i]:
+                copy.start()
+            pass_on(i)
+        project(x * 2 + which)
+    for c in range(PARTS):
+        ty[c] = collect(c).astype(BF)
+        cross(c).start()
+    for c in range(PARTS):
+        total = collect(PARTS + c)
+        cross(c).wait_recv()
+        out[c * part : (c + 1) * part, :] = (total + ry[c].astype(jnp.float32)).astype(BF)
+
+    for i in range(2 * PARTS):
+        for copy in first[i] + direct[i] + second[i]:
+            copy.wait_send()
+    for c in range(PARTS):
+        cross(c).wait_send()
 
     for g in heads:
         swap(g).wait_send()
@@ -307,181 +479,45 @@
                 fixed_copy(q, g).wait_send()
 
 
-def gather(owners, k, v):
+def layer(owners, pattern, q, k, v, w):
     dma = pltpu.SemaphoreType.DMA
+    width = LH * HD
     whole = pltpu.VMEM((HK, REF, HD), BF)
     hop = pltpu.VMEM((NZ // 2, LH, 2, PIECE, HD), BF)
+    part = TOK // PARTS
+    halves = pltpu.VMEM((2 * PARTS, part // 2, width), BF)
+    fulls = pltpu.VMEM((2 * PARTS, part, width), BF)
+    pairs = pltpu.VMEM((PARTS, part, width), BF)
+    column = pltpu.VMEM((LH, TOK, 1), jnp.float32)
+    hbm = pl.BlockSpec(memory_space=pl.ANY)
     return pl.pallas_call(
-        gather_kernel,
-        out_shape=jax.ShapeDtypeStruct((HK, PAD, HD), BF),
-        in_specs=[SMEM, VMEM, VMEM],
+        layer_kernel,
+        out_shape=jax.ShapeDtypeStruct((TOK, width), BF),
+        in_specs=[SMEM, SMEM, hbm, hbm, hbm, hbm],
         out_specs=VMEM,
         scratch_shapes=[
+            pltpu.VMEM((HK, PAD, HD), BF), pltpu.VMEM((TOK, width), BF),
+            pltpu.VMEM((2 * NX, width, width), BF),
             whole, whole, whole, hop, hop, hop, hop,
             pltpu.VMEM((HK, PIECE, HD), BF), pltpu.VMEM((NY - 1, LH, 2, PIECE, HD), BF),
+            pltpu.VMEM((TOK, PAD - OWN), jnp.float32), pltpu.VMEM((TOK, width), BF),
+            pltpu.VMEM((LH, TOK, HD), jnp.float32), column, column,
+            pltpu.VMEM((2 * NX, TOK, width), BF),
+            halves, halves, halves, halves, fulls, fulls, pairs, pairs,
             dma((6, LH)), dma((6, LH)), dma((2, LH)), dma((2, NZ // 2, LH)), dma((2, NZ // 2, LH)),
             dma((2, NZ, LH)), dma((2, NY, LH)), dma((2, NY, LH)),
             dma((2, NZ // 2, LH)), dma((2, NZ // 2, LH)), dma((2, LH)),
+            dma((HK,)), dma((2 * NX,)), dma, dma((6, 2 * PARTS)), dma((6, 2 * PARTS)), dma((2, PARTS)),
         ],
         compiler_params=pltpu.CompilerParams(
-            collective_id=0, has_side_effects=True, vmem_limit_bytes=40 << 20
+            collective_id=0, has_side_effects=True, vmem_limit_bytes=56 << 20
         ),
-        name="gather_keys",
-    )(owners, k, v)
-
-
-def attend_kernel(pattern_ref, q_ref, kv, w_ref, out, scores, att):
-    position = lax.broadcasted_iota(jnp.int32, (1, PAD), 1)
-    bias = jnp.where(position >= KEYS, NEG, 0.0)
-    for col in range(2 * REACH):
-        low = HALO + col * TOK
-        closed = jnp.where(pattern_ref[0, col] != 0, 0.0, NEG)
-        bias = bias + jnp.where((position >= low) & (position < low + TOK), closed, 0.0)
-    scale = HD ** -0.5
-    for h in range(LH):
-        q = q_ref[:, h * HD : (h + 1) * HD]
-        peak = jnp.full((TOK, HD), NEG, jnp.float32)
-        for t in range(PAD // 256):
-            keys = kv[2 * h, t * 256 : (t + 1) * 256, :]
-            sc = lax.dot_general(
-                q, keys, (((1,), (1,)), ((), ())), preferred_element_type=jnp.float32
-            )
-            sc = sc * scale + bias[:, t * 256 : (t + 1) * 256]
-            scores[:, t * 256 : (t + 1) * 256] = sc
-            peak = jnp.maximum(peak, jnp.maximum(sc[:, :128], sc[:, 128:]))
-        top = jnp.max(peak, axis=1, keepdims=True)
-        total = jnp.zeros((TOK, HD), jnp.float32)
-        acc = jnp.zeros((TOK, HD), jnp.float32)
-        for t in range(PAD // 256):
-            w = jnp.exp(scores[:, t * 256 : (t + 1) * 256] - top)
-            total = total + (w[:, :128] + w[:, 128:])
-            acc = acc + jnp.dot(
-                w.astype(BF), kv[2 * h + 1, t * 256 : (t + 1) * 256, :],
-                preferred_element_type=jnp.float32,
-            )
-        total = jnp.sum(total, axis=1, keepdims=True)
-        att[:, h * HD : (h + 1) * HD] = (acc / total).astype(BF)
-    width = LH * HD
-    for b in range(2 * NX):
-        out[b] = jnp.dot(
-            att[...], w_ref[:, b * width : (b + 1) * width], preferred_element_type=jnp.float32
-        ).astype(BF)
-
-
-def attend(pattern, q, kv, w):
-    return pl.pallas_call(
-        attend_kernel,
-        out_shape=jax.ShapeDtypeStruct((2 * NX, TOK, LH * HD), BF),
-        in_specs=[SMEM, VMEM, VMEM, VMEM],
-        out_specs=VMEM,
-        scratch_shapes=[pltpu.VMEM((TOK, PAD), jnp.float32), pltpu.VMEM((TOK, LH * HD), BF)],
-        compiler_params=pltpu.CompilerParams(vmem_limit_bytes=48 << 20),
-        name="attend",
-    )(pattern, q, kv, w)
-
-
-def mix_kernel(p, out, r1p, r1m, t2p, t2m, r2p, r2m, ty, ry, s_sem, r_sem, y_sem):
-    h = lax.axis_index("head")
-    x = h // 2
-    y = lax.rem(h, 2)
-    xn = lax.rem(x + 1, NX)
-    xp = lax.rem(x + NX - 1, NX)
-    xo = lax.rem(x + 2, NX)
-    nxt = xn * 2 + y
-    prv = xp * 2 + y
-    pair = x * 2 + 1 - y
-    barrier = pltpu.get_barrier_semaphore()
-    for peer in (nxt, prv, pair):
-        pl.semaphore_signal(barrier, inc=1, device_id={"head": peer}, device_id_type=MESH)
-    pl.semaphore_wait(barrier, 3)
-    half = TOK // 2
-    top, bottom = slice(0, half), slice(half, TOK)
-
-    def copy(kind, i, src, dst, peer):
-        return pltpu.make_async_remote_copy(
-            src_ref=src, dst_ref=dst, send_sem=s_sem.at[kind, i], recv_sem=r_sem.at[kind, i],
-            device_id={"head": peer}, device_id_type=MESH,
-        )
-
-    def cross(i):
-        return pltpu.make_async_remote_copy(
-            src_ref=ty, dst_ref=ry, send_sem=y_sem.at[0], recv_sem=y_sem.at[1],
-            device_id={"head": pair}, device_id_type=MESH,
-        )
-
-    sides = (1 - y, y)
-    stage1 = []
-    direct = []
-    for i, side in enumerate(sides):
-        far = xo * 2 + side
-        stage1.append((
-            copy(0, i, p.at[far, top], r1p.at[i], nxt),
-            copy(1, i, p.at[far, bottom], r1m.at[i], prv),
-        ))
-        direct.append((
-            copy(2, i, p.at[xn * 2 + side, bottom], r2p.at[i, bottom], nxt),
-            copy(3, i, p.at[xp * 2 + side, top], r2m.at[i, top], prv),
-        ))
-    for i in range(2):
-        for c in stage1[i]:
-            c.start()
-        for c in direct[i]:
-            c.start()
-    stage2 = []
-    for i, side in enumerate(sides):
-        stage1[i][0].wait_recv()
-        t2p[i] = p[xn * 2 + side, top] + r1p[i]
-        a = copy(4, i, t2p.at[i], r2p.at[i, top], nxt)
-        a.start()
-        stage1[i][1].wait_recv()
-        t2m[i] = p[xp * 2 + side, bottom] + r1m[i]
-        b = copy(5, i, t2m.at[i], r2m.at[i, bottom], prv)
-        b.start()
-        stage2.append((a, b))
-    for i, side in enumerate(sides):
-        for c in direct[i] + stage2[i]:
-            c.wait_recv()
-        total = (
-            p[x * 2 + side].astype(jnp.float32)
-            + r2p[i].astype(jnp.float32)
-            + r2m[i].astype(jnp.float32)
-        )
-        if i == 0:
-            ty[...] = total.astype(BF)
-            cross(0).start()
-        else:
-            cross(0).wait_recv()
-            out[...] = (total + ry[...].astype(jnp.float32)).astype(BF)
-    for i in range(2):
-        for c in stage1[i] + direct[i] + stage2[i]:
-            c.wait_send()
-    cross(0).wait_send()
-
-
-def mix(p):
-    dma = pltpu.SemaphoreType.DMA
-    width = LH * HD
-    halfs = pltpu.VMEM((2, TOK // 2, width), BF)
-    fulls = pltpu.VMEM((2, TOK, width), BF)
-    one = pltpu.VMEM((TOK, width), BF)
-    return pl.pallas_call(
-        mix_kernel,
-        out_shape=jax.ShapeDtypeStruct((TOK, width), BF),
-        in_specs=[VMEM],
-        out_specs=VMEM,
-        scratch_shapes=[
-            halfs, halfs, halfs, halfs, fulls, fulls, one, one, dma((6, 2)), dma((6, 2)), dma((2,)),
-        ],
-        compiler_params=pltpu.CompilerParams(
-            collective_id=1, has_side_effects=True, vmem_limit_bytes=32 << 20
-        ),
-        name="mix_heads",
-    )(p)
+        name="layer",
+    )(owners, pattern, q, k, v, w)
 
 
 def body(query_rows, key_rows, value_rows, pattern, owners, out_weight):
-    kv = gather(owners, key_rows, value_rows)
-    return mix(attend(pattern, query_rows, kv, out_weight))
+    return layer(owners, pattern, query_rows, key_rows, value_rows, out_weight)
 
 
 def solution(mesh):

time: 112 us -> 97.4 us (0.87)
  the two profiles are of different devices: /device:TPU:49 before, /device:TPU:25 now
where the time goes in v3:
time: 97.4 us; the launch traced here: 97.2 us
  Pallas kernels  95.5 us (98%)
  local copies, waits for them, and re-layouts  1.66 us (2%)
    pallas_call x1, Pallas kernels, layer(): pl.pallas_call(layer_kernel, out_shape=jax.ShapeDtypeStruct((TOK, width),...  95.5 us

profile of v3, /device:TPU:25, one launch (start us, length us, event | category | flops | bytes accessed | tf_op | source)
XLA Modules:
  0.0 97.2 jit_solution(6348678029804418695)
XLA Ops:
  0.0 95.5 %layer.1 = bf16[320,384]{1,0:T(8,128)(2,1)} custom-call(s32[4]{0:T(128)} %owners_ref.1, s32[1,6]{1,0:T(1,128)} %pattern_ref.1, bf16[320,384]{1,0:T(8,128)(2,1)} %q_hbm.1, bf16[320,384]{1,0:T(8,128)(2,1)} %k_hbm.1, bf16[320,384]{1,0:T(8,128)(2,1)} %v_hbm.1, bf16[384,3072]{1,0:T(8,128)(2,1)} %w_hbm.1), custom_call_target="tpu_custom_call" | custom-call | tf_op jit(solution)/shard_map/layer/pallas_call | solution.py:493
  95.5 1.7 %copy.8 = bf16[320,384]{1,0:T(8,128)(2,1)} copy(bf16[320,384]{1,0:T(8,128)(2,1)} %layer.1) | data formatting | bytes 491520

commit v4 on v3

--- a/solution.py
+++ b/solution.py
@@ -25,6 +25,18 @@
 NEG = -1e30
 TILE = 256
 PARTS = 2
+PACE = (
+    (("own", 2), ("spread",)),
+    (("own", 3),),
+    (("own", 4), ("here",), ("fixed", 0)),
+    (("own", 5), ("fixed", 1), ("on", 0)),
+    (("fixed", 2), ("on", 1), ("on", 2)),
+    (("fixed", 3), ("on", 3)),
+    (("on", 4), ("near", 0)),
+    (("on", 5), ("near", 1)),
+    (("near", 2),),
+    (),
+)
 VMEM = pl.BlockSpec(memory_space=pltpu.VMEM)
 SMEM = pl.BlockSpec(memory_space=pltpu.SMEM)
 BF = jnp.bfloat16
@@ -34,7 +46,7 @@
     owners_ref, pattern_ref, q_hbm, k_hbm, v_hbm, w_hbm, out,
     kv, qb, wb, mine, msend, mrecv, ps, pr, ss, sr, ysend, yr,
     scores, att, acc1, top1, total1, p, r1p, r1m, t2p, t2m, r2p, r2m, ty, ry,
-    hs_sem, hr_sem, m_sem, p_sem, s_sem, x_sem, y_sem, ys_sem, a_sem, b_sem, f_sem,
+    hs_sem, hr_sem, m_sem, p_sem, s_sem, x_sem, y_sem, ys_sem, a_sem, b_sem, fa_sem, fb_sem, f_sem,
     in_sem, w_sem, q_sem, mix_s, mix_r, c_sem,
 ):
     s = lax.axis_index("seq")
@@ -67,6 +79,7 @@
         yy = jnp.where(core == 0, yy, NY - 1 - yy)
         return (yy * NZ + zz) * 2 + core
 
+    far, near = NZ // 2, NZ // 2 - 1
     ahead = at(py, pz + 1)
     behind = at(py, pz - 1)
 
@@ -141,34 +154,80 @@
         start = lax.rem(q + NZ, NZ) * PIECE
         return mine[2 * g : 2 * g + 2, pl.ds(pl.multiple_of(start, PIECE), PIECE), :]
 
-    def fixed_copy(q, g):
+    def fixed_rows(q):
+        start = base + lax.rem(q + NZ, NZ) * 2 * PIECE + PIECE
+        return kv.at[:, pl.ds(pl.multiple_of(start, PIECE), PIECE)]
+
+    def fixed_copy(q):
         return remote(
-            kv.at[2 * g : 2 * g + 2, OWN + q * PIECE : OWN + (q + 1) * PIECE],
-            piece(g, q, PIECE, PIECE), x_sem.at[0, q, g], x_sem.at[1, 0, g], at(0, q),
+            kv.at[:, OWN + q * PIECE : OWN + (q + 1) * PIECE], fixed_rows(q),
+            x_sem.at[0, q], x_sem.at[1, 0], at(0, q),
         )
 
     def y_copy(d, g):
         return remote(planes(ysend, g), yr.at[d - 1, g], y_sem.at[0, d, g], y_sem.at[1, d, g], at(py + d, pz))
 
-    def y_fixed(d, g):
-        part = piece(g, pz, PIECE, PIECE)
-        return remote(part, part, ys_sem.at[0, d, g], ys_sem.at[1, 0, g], at(py + d, pz))
+    def y_fixed(d):
+        return remote(fixed_rows(pz), fixed_rows(pz), ys_sem.at[0, d], ys_sem.at[1, 0], at(py + d, pz))
 
     def around(j, g):
-        part = piece(g, pz - j, 0, 2 * PIECE)
+        part = piece(g, pz - j, 0, PIECE)
         return remote(part, part, a_sem.at[0, j, g], a_sem.at[1, j, g], ahead)
 
     def around_arrived(j, g):
-        part = piece(g, pz - j - 1, 0, 2 * PIECE)
+        part = piece(g, pz - j - 1, 0, PIECE)
         remote(part, part, a_sem.at[0, j, g], a_sem.at[1, j, g], ahead).wait_recv()
 
     def back(j, g):
-        part = piece(g, pz + j, 0, 2 * PIECE)
+        part = piece(g, pz + j, 0, PIECE)
         return remote(part, part, b_sem.at[0, j, g], b_sem.at[1, j, g], behind)
 
     def back_arrived(j, g):
-        part = piece(g, pz + j + 1, 0, 2 * PIECE)
+        part = piece(g, pz + j + 1, 0, PIECE)
         remote(part, part, b_sem.at[0, j, g], b_sem.at[1, j, g], behind).wait_recv()
+
+    def fixed_around(j):
+        part = fixed_rows(pz - j)
+        return remote(part, part, fa_sem.at[0, j], fa_sem.at[1, j], ahead)
+
+    def fixed_back(j):
+        part = fixed_rows(pz + j)
+        return remote(part, part, fb_sem.at[0, j], fb_sem.at[1, j], behind)
+
+    def fixed_start(j):
+        if j > 0:
+            part = fixed_rows(pz - j)
+            remote(part, part, fa_sem.at[0, j - 1], fa_sem.at[1, j - 1], ahead).wait_recv()
+        fixed_around(j).start()
+        if j < near:
+            if j > 0:
+                part = fixed_rows(pz + j)
+                remote(part, part, fb_sem.at[0, j - 1], fb_sem.at[1, j - 1], behind).wait_recv()
+            fixed_back(j).start()
+
+    def fixed_finish():
+        part = fixed_rows(pz - far)
+        remote(part, part, fa_sem.at[0, far - 1], fa_sem.at[1, far - 1], ahead).wait_recv()
+        if near > 0:
+            part = fixed_rows(pz + near)
+            remote(part, part, fb_sem.at[0, near - 1], fb_sem.at[1, near - 1], behind).wait_recv()
+
+    def fixed_spread():
+        @pl.when(py == 0)
+        def _():
+            @pl.when(pz > 0)
+            def _():
+                part = fixed_rows(pz)
+                remote(part, part, x_sem.at[0, 0], x_sem.at[1, 0], ahead).wait_recv()
+
+            for d in range(1, NY):
+                y_fixed(d).start()
+
+    def fixed_here():
+        @pl.when(py > 0)
+        def _():
+            part = fixed_rows(pz)
+            remote(part, part, ys_sem.at[0, 0], ys_sem.at[1, 0], ahead).wait_recv()
 
     def share(g):
         part = kv.at[2 * g : 2 * g + 2, pl.ds(pl.multiple_of(base, PIECE), 2 * REF)]
@@ -178,40 +237,40 @@
         part = kv.at[2 * g : 2 * g + 2, pl.ds(pl.multiple_of(2 * REF - base, PIECE), 2 * REF)]
         remote(part, part, f_sem.at[0, g], f_sem.at[1, g], partner).wait_recv()
 
-    def halo_rows(g, col):
-        return kv.at[2 * g : 2 * g + 2, pl.ds(pl.multiple_of(HALO + col * TOK, 16), TOK)]
-
-    def halo_copy(kind, src, g, col, peer):
-        return remote(src, halo_rows(g, col), hs_sem.at[kind, g], hr_sem.at[col, g], peer)
-
-    def own_rows(g):
-        return kv.at[2 * g : 2 * g + 2, OWN:HALO]
-
-    def halo_sends(g):
+    def halo_rows(hk, col):
+        return kv.at[hk, pl.ds(pl.multiple_of(HALO + col * TOK, 16), TOK)]
+
+    def halo_copy(kind, src, hk, col, peer):
+        return remote(src, halo_rows(hk, col), hs_sem.at[kind, hk], hr_sem.at[col, hk], peer)
+
+    def own_rows(hk):
+        return kv.at[hk, OWN:HALO]
+
+    def halo_sends(hk):
         return (
-            halo_copy(0, own_rows(g), g, 1, right),
-            halo_copy(1, own_rows(g), g, 4, left),
-            halo_copy(2, own_rows(g), g, 2 + core, partner),
-        )
-
-    def forwards(g):
+            halo_copy(0, own_rows(hk), hk, 1, right),
+            halo_copy(1, own_rows(hk), hk, 4, left),
+            halo_copy(2, own_rows(hk), hk, 2 + core, partner),
+        )
+
+    def forwards(hk):
         return (
-            halo_copy(3, halo_rows(g, 1), g, 2 * core, partner),
-            halo_copy(4, halo_rows(g, 4), g, 3 + 2 * core, partner),
-            halo_copy(5, halo_rows(g, 4 - 3 * core), g, 5 - 5 * core, extra),
-        )
-
-    def halo_wait(g, col):
-        halo_copy(0, own_rows(g), g, col, right).wait_recv()
-
-    def halo_start(g):
-        for copy in halo_sends(g):
+            halo_copy(5, halo_rows(hk, 4 - 3 * core), hk, 5 - 5 * core, extra),
+            halo_copy(3, halo_rows(hk, 1), hk, 2 * core, partner),
+            halo_copy(4, halo_rows(hk, 4), hk, 3 + 2 * core, partner),
+        )
+
+    def halo_wait(hk, col):
+        halo_copy(0, own_rows(hk), hk, col, right).wait_recv()
+
+    def halo_start(hk):
+        for copy in halo_sends(hk):
             copy.start()
 
-    def halo_forward(g):
-        halo_wait(g, 1)
-        halo_wait(g, 4)
-        for copy in forwards(g):
+    def halo_forward(hk):
+        halo_wait(hk, 1)
+        halo_wait(hk, 4)
+        for copy in forwards(hk):
             copy.start()
 
     position = lax.broadcasted_iota(jnp.int32, (1, PAD - OWN), 1) + OWN
@@ -250,7 +309,8 @@
     def near_part(h):
         for col in range(2 * REACH):
             if col not in (1, 4):
-                halo_wait(h, col)
+                halo_wait(2 * h, col)
+                halo_wait(2 * h + 1, col)
         top, total, acc = segment(h, OWN, PAD)
         top1[h] = top
         total1[h] = total
@@ -266,22 +326,24 @@
 
     source = (pz == 0) & (py == 0)
     heads = range(LH)
+    step_actions = {
+        "own": halo_start, "on": halo_forward, "near": near_part, "spread": fixed_spread,
+        "here": fixed_here, "fixed": fixed_start,
+    }
     for g in heads:
         swap(g).start()
 
     @pl.when(source)
     def _():
-        for g in heads:
-            for q in range(1, NZ):
-                fixed_copy(q, g).start()
-            part = kv[2 * g : 2 * g + 2, OWN : OWN + PIECE, :]
-            piece(g, 0, PIECE, PIECE)[...] = part
+        for q in range(1, NZ):
+            fixed_copy(q).start()
+        fixed_rows(0)[...] = kv[:, OWN : OWN + PIECE, :]
 
     halo_start(0)
+    halo_start(1)
     query_load.start()
     for load in weight_loads:
         load.start()
-    far, near = NZ // 2, NZ // 2 - 1
     for j in range(far):
         for g in heads:
             if j == 0:
@@ -300,18 +362,8 @@
                     s_copy(j - 1, g).wait_recv()
                     ss[j, g] = mine_rows(g, pz - near + j) + sr[j - 1, g]
                     s_copy(j, g).start()
-        if j == 1:
-            halo_start(1)
-        if j == 2:
-            halo_start(2)
-            halo_forward(0)
-        if j == 3:
-            halo_forward(1)
-    if far <= 2:
-        halo_start(2)
-        halo_forward(0)
-    if far <= 3:
-        halo_forward(1)
+        for action in PACE[j]:
+            step_actions[action[0]](*action[1:])
     for g in heads:
         total = mine_rows(g, pz)
         if near > 0:
@@ -321,34 +373,20 @@
         ysend[2 * g : 2 * g + 2] = total + pr[far - 1, g]
         for d in range(1, NY):
             y_copy(d, g).start()
-
-        @pl.when(py == 0)
-        def _():
-            @pl.when(pz > 0)
-            def _():
-                part = piece(g, pz, PIECE, PIECE)
-                remote(part, part, x_sem.at[0, 0, g], x_sem.at[1, 0, g], ahead).wait_recv()
-
-            for d in range(1, NY):
-                y_fixed(d, g).start()
-
-    halo_forward(2)
+    for action in PACE[far]:
+        step_actions[action[0]](*action[1:])
     for g in heads:
         total = ysend[2 * g : 2 * g + 2]
         for d in range(1, NY):
             y_copy(d, g).wait_recv()
             total = total + yr[d - 1, g]
         piece(g, pz, 0, PIECE)[...] = total
-
-        @pl.when(py > 0)
-        def _():
-            part = piece(g, pz, PIECE, PIECE)
-            remote(part, part, ys_sem.at[0, 0, g], ys_sem.at[1, 0, g], ahead).wait_recv()
-
         around(0, g).start()
         if near > 0:
             back(0, g).start()
     query_load.wait()
+    for action in PACE[far + 1]:
+        step_actions[action[0]](*action[1:])
     for j in range(1, far):
         for g in heads:
             around_arrived(j - 1, g)
@@ -356,18 +394,19 @@
             if j < near:
                 back_arrived(j - 1, g)
                 back(j, g).start()
-        near_part(j - 1)
-    for h in range(far - 1, LH):
-        near_part(h)
+        for action in PACE[far + 1 + j]:
+            step_actions[action[0]](*action[1:])
+    fixed_finish()
     for g in heads:
         around_arrived(far - 1, g)
         if near > 0:
             back_arrived(near - 1, g)
         share(g).start()
+    for action in PACE[2 * far + 1]:
+        step_actions[action[0]](*action[1:])
     for g in heads:
         shared(g)
         far_part(g)
-
     for load in weight_loads:
         load.wait()
 
@@ -465,18 +504,23 @@
             back(j, g).wait_send()
         for d in range(1, NY):
             y_copy(d, g).wait_send()
-        for copy in halo_sends(g) + forwards(g):
+    for j in range(far):
+        fixed_around(j).wait_send()
+    for j in range(near):
+        fixed_back(j).wait_send()
+    for hk in range(HK):
+        for copy in halo_sends(hk) + forwards(hk):
             copy.wait_send()
 
-        @pl.when(py == 0)
-        def _():
-            for d in range(1, NY):
-                y_fixed(d, g).wait_send()
-
-        @pl.when(source)
-        def _():
-            for q in range(1, NZ):
-                fixed_copy(q, g).wait_send()
+    @pl.when(py == 0)
+    def _():
+        for d in range(1, NY):
+            y_fixed(d).wait_send()
+
+    @pl.when(source)
+    def _():
+        for q in range(1, NZ):
+            fixed_copy(q).wait_send()
 
 
 def layer(owners, pattern, q, k, v, w):
@@ -504,9 +548,9 @@
             pltpu.VMEM((LH, TOK, HD), jnp.float32), column, column,
             pltpu.VMEM((2 * NX, TOK, width), BF),
             halves, halves, halves, halves, fulls, fulls, pairs, pairs,
-            dma((6, LH)), dma((6, LH)), dma((2, LH)), dma((2, NZ // 2, LH)), dma((2, NZ // 2, LH)),
-            dma((2, NZ, LH)), dma((2, NY, LH)), dma((2, NY, LH)),
-            dma((2, NZ // 2, LH)), dma((2, NZ // 2, LH)), dma((2, LH)),
+            dma((6, HK)), dma((6, HK)), dma((2, LH)), dma((2, NZ // 2, LH)), dma((2, NZ // 2, LH)),
+            dma((2, NZ)), dma((2, NY, LH)), dma((2, NY)),
+            dma((2, NZ // 2, LH)), dma((2, NZ // 2, LH)), dma((2, NZ // 2)), dma((2, NZ // 2)), dma((2, LH)),
             dma((HK,)), dma((2 * NX,)), dma, dma((6, 2 * PARTS)), dma((6, 2 * PARTS)), dma((2, PARTS)),
         ],
         compiler_params=pltpu.CompilerParams(

time: 97.4 us -> 94.5 us (0.970)
  the two profiles are of different devices: /device:TPU:25 before, /device:TPU:1 now
where the time goes in v4:
time: 94.5 us; the launch traced here: 94.3 us
  Pallas kernels  92.6 us (98%)
  local copies, waits for them, and re-layouts  1.66 us (2%)
    pallas_call x1, Pallas kernels, layer(): pl.pallas_call(layer_kernel, out_shape=jax.ShapeDtypeStruct((TOK, width),...  92.6 us

profile of v4, /device:TPU:1, one launch (start us, length us, event | category | flops | bytes accessed | tf_op | source)
XLA Modules:
  0.0 94.3 jit_solution(15549332370987139422)
XLA Ops:
  0.0 92.6 %layer.1 = bf16[320,384]{1,0:T(8,128)(2,1)} custom-call(s32[4]{0:T(128)} %owners_ref.1, s32[1,6]{1,0:T(1,128)} %pattern_ref.1, bf16[320,384]{1,0:T(8,128)(2,1)} %q_hbm.1, bf16[320,384]{1,0:T(8,128)(2,1)} %k_hbm.1, bf16[320,384]{1,0:T(8,128)(2,1)} %v_hbm.1, bf16[384,3072]{1,0:T(8,128)(2,1)} %w_hbm.1), custom_call_target="tpu_custom_call" | custom-call | tf_op jit(solution)/shard_map/layer/pallas_call | solution.py:537
  92.6 1.7 %copy.8 = bf16[320,384]{1,0:T(8,128)(2,1)} copy(bf16[320,384]{1,0:T(8,128)(2,1)} %layer.1) | data formatting | bytes 491520

commit v5 on v4

--- a/solution.py
+++ b/solution.py
@@ -24,17 +24,19 @@
 PAD = -(-KEYS // 256) * 256
 NEG = -1e30
 TILE = 256
+GROUPS = 1
+PER = HK // GROUPS
 PARTS = 2
 PACE = (
     (("own", 2), ("spread",)),
     (("own", 3),),
     (("own", 4), ("here",), ("fixed", 0)),
-    (("own", 5), ("fixed", 1), ("on", 0)),
-    (("fixed", 2), ("on", 1), ("on", 2)),
-    (("fixed", 3), ("on", 3)),
-    (("on", 4), ("near", 0)),
+    (("own", 5), ("fixed", 1), ("on", 0), ("on", 1)),
+    (("fixed", 2), ("on", 2), ("on", 3), ("query",), ("near", 0)),
+    (("fixed", 3), ("on", 4)),
     (("on", 5), ("near", 1)),
     (("near", 2),),
+    (("fixed_part",),),
     (),
 )
 VMEM = pl.BlockSpec(memory_space=pltpu.VMEM)
@@ -133,7 +135,7 @@
         )
 
     def planes(ref, g):
-        return ref.at[2 * g : 2 * g + 2]
+        return ref.at[PER * g : PER * g + PER]
 
     def swap(g):
         return remote(planes(msend, g), planes(mrecv, g), m_sem.at[0, g], m_sem.at[1, g], partner)
@@ -144,18 +146,18 @@
     def s_copy(j, g):
         return remote(ss.at[j, g], sr.at[j, g], s_sem.at[0, j, g], s_sem.at[1, j, g], behind)
 
-    base = core * 2 * REF
-
-    def piece(g, q, first, count):
-        start = base + lax.rem(q + NZ, NZ) * 2 * PIECE + first
-        return kv.at[2 * g : 2 * g + 2, pl.ds(pl.multiple_of(start, PIECE), count)]
+    base = core * REF
+
+    def piece(g, q):
+        start = base + lax.rem(q + NZ, NZ) * PIECE
+        return kv.at[PER * g : PER * g + PER, pl.ds(pl.multiple_of(start, PIECE), PIECE)]
 
     def mine_rows(g, q):
         start = lax.rem(q + NZ, NZ) * PIECE
-        return mine[2 * g : 2 * g + 2, pl.ds(pl.multiple_of(start, PIECE), PIECE), :]
+        return mine[PER * g : PER * g + PER, pl.ds(pl.multiple_of(start, PIECE), PIECE), :]
 
     def fixed_rows(q):
-        start = base + lax.rem(q + NZ, NZ) * 2 * PIECE + PIECE
+        start = 2 * REF + base + lax.rem(q + NZ, NZ) * PIECE
         return kv.at[:, pl.ds(pl.multiple_of(start, PIECE), PIECE)]
 
     def fixed_copy(q):
@@ -171,19 +173,19 @@
         return remote(fixed_rows(pz), fixed_rows(pz), ys_sem.at[0, d], ys_sem.at[1, 0], at(py + d, pz))
 
     def around(j, g):
-        part = piece(g, pz - j, 0, PIECE)
+        part = piece(g, pz - j)
         return remote(part, part, a_sem.at[0, j, g], a_sem.at[1, j, g], ahead)
 
     def around_arrived(j, g):
-        part = piece(g, pz - j - 1, 0, PIECE)
+        part = piece(g, pz - j - 1)
         remote(part, part, a_sem.at[0, j, g], a_sem.at[1, j, g], ahead).wait_recv()
 
     def back(j, g):
-        part = piece(g, pz + j, 0, PIECE)
+        part = piece(g, pz + j)
         return remote(part, part, b_sem.at[0, j, g], b_sem.at[1, j, g], behind)
 
     def back_arrived(j, g):
-        part = piece(g, pz + j + 1, 0, PIECE)
+        part = piece(g, pz + j + 1)
         remote(part, part, b_sem.at[0, j, g], b_sem.at[1, j, g], behind).wait_recv()
 
     def fixed_around(j):
@@ -199,18 +201,18 @@
             part = fixed_rows(pz - j)
             remote(part, part, fa_sem.at[0, j - 1], fa_sem.at[1, j - 1], ahead).wait_recv()
         fixed_around(j).start()
+        share(1, -j).start()
+        if j <= near and j > 0:
+            part = fixed_rows(pz + j)
+            remote(part, part, fb_sem.at[0, j - 1], fb_sem.at[1, j - 1], behind).wait_recv()
+            share(1, j).start()
         if j < near:
-            if j > 0:
-                part = fixed_rows(pz + j)
-                remote(part, part, fb_sem.at[0, j - 1], fb_sem.at[1, j - 1], behind).wait_recv()
             fixed_back(j).start()
 
     def fixed_finish():
         part = fixed_rows(pz - far)
         remote(part, part, fa_sem.at[0, far - 1], fa_sem.at[1, far - 1], ahead).wait_recv()
-        if near > 0:
-            part = fixed_rows(pz + near)
-            remote(part, part, fb_sem.at[0, near - 1], fb_sem.at[1, near - 1], behind).wait_recv()
+        share(1, -far).start()
 
     def fixed_spread():
         @pl.when(py == 0)
@@ -229,13 +231,18 @@
             part = fixed_rows(pz)
             remote(part, part, ys_sem.at[0, 0], ys_sem.at[1, 0], ahead).wait_recv()
 
-    def share(g):
-        part = kv.at[2 * g : 2 * g + 2, pl.ds(pl.multiple_of(base, PIECE), 2 * REF)]
-        return remote(part, part, f_sem.at[0, g], f_sem.at[1, g], partner)
-
-    def shared(g):
-        part = kv.at[2 * g : 2 * g + 2, pl.ds(pl.multiple_of(2 * REF - base, PIECE), 2 * REF)]
-        remote(part, part, f_sem.at[0, g], f_sem.at[1, g], partner).wait_recv()
+    def share(kind, off):
+        start = (2 * kind + core) * REF + lax.rem(pz + off + NZ, NZ) * PIECE
+        part = kv.at[:, pl.ds(pl.multiple_of(start, PIECE), PIECE)]
+        return remote(part, part, f_sem.at[0, kind, off + far], f_sem.at[1, kind, off + far], partner)
+
+    def shared(kind):
+        for off in range(-far, near + 1):
+            start = (2 * kind + 1 - core) * REF + lax.rem(2 * NZ - 1 - pz + off, NZ) * PIECE
+            part = kv.at[:, pl.ds(pl.multiple_of(start, PIECE), PIECE)]
+            remote(
+                part, part, f_sem.at[0, kind, off + far], f_sem.at[1, kind, off + far], partner
+            ).wait_recv()
 
     def halo_rows(hk, col):
         return kv.at[hk, pl.ds(pl.multiple_of(HALO + col * TOK, 16), TOK)]
@@ -316,21 +323,34 @@
         total1[h] = total
         acc1[h] = acc
 
-    def far_part(h):
-        top, total, acc = segment(h, 0, OWN)
+    def joined(h, first, last):
+        top, total, acc = segment(h, first, last)
         best = jnp.maximum(top, top1[h])
         new = jnp.exp(top - best)
         old = jnp.exp(top1[h] - best)
-        whole = total * new + total1[h] * old
-        att[:, h * HD : (h + 1) * HD] = ((acc * new + acc1[h] * old) / whole).astype(BF)
+        return best, total * new + total1[h] * old, acc * new + acc1[h] * old
+
+    def fixed_part():
+        fixed_finish()
+        shared(1)
+        for h in range(LH):
+            best, total, acc = joined(h, 2 * REF, OWN)
+            top1[h] = best
+            total1[h] = total
+            acc1[h] = acc
+
+    def last_part(h):
+        best, total, acc = joined(h, 0, 2 * REF)
+        att[:, h * HD : (h + 1) * HD] = (acc / total).astype(BF)
 
     source = (pz == 0) & (py == 0)
     heads = range(LH)
+    groups = range(GROUPS)
     step_actions = {
         "own": halo_start, "on": halo_forward, "near": near_part, "spread": fixed_spread,
-        "here": fixed_here, "fixed": fixed_start,
+        "here": fixed_here, "fixed": fixed_start, "fixed_part": fixed_part, "query": query_load.wait,
     }
-    for g in heads:
+    for g in groups:
         swap(g).start()
 
     @pl.when(source)
@@ -345,10 +365,10 @@
     for load in weight_loads:
         load.start()
     for j in range(far):
-        for g in heads:
+        for g in groups:
             if j == 0:
                 swap(g).wait_recv()
-                mine[2 * g : 2 * g + 2] = mine[2 * g : 2 * g + 2] + mrecv[2 * g : 2 * g + 2]
+                mine[PER * g : PER * g + PER] = mine[PER * g : PER * g + PER] + mrecv[PER * g : PER * g + PER]
                 ps[0, g] = mine_rows(g, pz + far)
                 p_copy(0, g).start()
                 if near > 0:
@@ -364,49 +384,49 @@
                     s_copy(j, g).start()
         for action in PACE[j]:
             step_actions[action[0]](*action[1:])
-    for g in heads:
+    for g in groups:
         total = mine_rows(g, pz)
         if near > 0:
             s_copy(near - 1, g).wait_recv()
             total = total + sr[near - 1, g]
         p_copy(far - 1, g).wait_recv()
-        ysend[2 * g : 2 * g + 2] = total + pr[far - 1, g]
+        ysend[PER * g : PER * g + PER] = total + pr[far - 1, g]
         for d in range(1, NY):
             y_copy(d, g).start()
     for action in PACE[far]:
         step_actions[action[0]](*action[1:])
-    for g in heads:
-        total = ysend[2 * g : 2 * g + 2]
+    for g in groups:
+        total = ysend[PER * g : PER * g + PER]
         for d in range(1, NY):
             y_copy(d, g).wait_recv()
             total = total + yr[d - 1, g]
-        piece(g, pz, 0, PIECE)[...] = total
+        piece(g, pz)[...] = total
         around(0, g).start()
         if near > 0:
             back(0, g).start()
-    query_load.wait()
+        share(0, 0).start()
     for action in PACE[far + 1]:
         step_actions[action[0]](*action[1:])
     for j in range(1, far):
-        for g in heads:
+        for g in groups:
             around_arrived(j - 1, g)
             around(j, g).start()
+            share(0, -j).start()
+            if j <= near:
+                back_arrived(j - 1, g)
+                share(0, j).start()
             if j < near:
-                back_arrived(j - 1, g)
                 back(j, g).start()
         for action in PACE[far + 1 + j]:
             step_actions[action[0]](*action[1:])
-    fixed_finish()
-    for g in heads:
+    for g in groups:
         around_arrived(far - 1, g)
-        if near > 0:
-            back_arrived(near - 1, g)
-        share(g).start()
+        share(0, -far).start()
     for action in PACE[2 * far + 1]:
         step_actions[action[0]](*action[1:])
-    for g in heads:
-        shared(g)
-        far_part(g)
+    shared(0)
+    for h in heads:
+        last_part(h)
     for load in weight_loads:
         load.wait()
 
@@ -465,23 +485,30 @@
             + r2m[i].astype(jnp.float32)
         )
 
-    for phase in range(2):
+    def launch(phase):
         which = items[phase * PARTS][0]
-        mineq = range(phase * PARTS, (phase + 1) * PARTS)
+        todo = range(phase * PARTS, (phase + 1) * PARTS)
         project(xo * 2 + which)
-        for i in mineq:
+        for i in todo:
             for copy in first[i]:
                 copy.start()
         project(xn * 2 + which)
         project(xp * 2 + which)
-        for i in mineq:
+        for i in todo:
             for copy in direct[i]:
                 copy.start()
-            pass_on(i)
-        project(x * 2 + which)
+
+    launch(0)
+    for i in range(PARTS):
+        pass_on(i)
+    launch(1)
+    project(x * 2 + 1 - side)
     for c in range(PARTS):
         ty[c] = collect(c).astype(BF)
         cross(c).start()
+    project(x * 2 + side)
+    for i in range(PARTS, 2 * PARTS):
+        pass_on(i)
     for c in range(PARTS):
         total = collect(PARTS + c)
         cross(c).wait_recv()
@@ -493,9 +520,11 @@
     for c in range(PARTS):
         cross(c).wait_send()
 
-    for g in heads:
+    for kind in range(2):
+        for off in range(-far, near + 1):
+            share(kind, off).wait_send()
+    for g in groups:
         swap(g).wait_send()
-        share(g).wait_send()
         for j in range(far):
             p_copy(j, g).wait_send()
             around(j, g).wait_send()
@@ -527,7 +556,7 @@
     dma = pltpu.SemaphoreType.DMA
     width = LH * HD
     whole = pltpu.VMEM((HK, REF, HD), BF)
-    hop = pltpu.VMEM((NZ // 2, LH, 2, PIECE, HD), BF)
+    hop = pltpu.VMEM((NZ // 2, GROUPS, PER, PIECE, HD), BF)
     part = TOK // PARTS
     halves = pltpu.VMEM((2 * PARTS, part // 2, width), BF)
     fulls = pltpu.VMEM((2 * PARTS, part, width), BF)
@@ -543,14 +572,14 @@
             pltpu.VMEM((HK, PAD, HD), BF), pltpu.VMEM((TOK, width), BF),
             pltpu.VMEM((2 * NX, width, width), BF),
             whole, whole, whole, hop, hop, hop, hop,
-            pltpu.VMEM((HK, PIECE, HD), BF), pltpu.VMEM((NY - 1, LH, 2, PIECE, HD), BF),
+            pltpu.VMEM((HK, PIECE, HD), BF), pltpu.VMEM((NY - 1, GROUPS, PER, PIECE, HD), BF),
             pltpu.VMEM((TOK, PAD - OWN), jnp.float32), pltpu.VMEM((TOK, width), BF),
             pltpu.VMEM((LH, TOK, HD), jnp.float32), column, column,
             pltpu.VMEM((2 * NX, TOK, width), BF),
             halves, halves, halves, halves, fulls, fulls, pairs, pairs,
-            dma((6, HK)), dma((6, HK)), dma((2, LH)), dma((2, NZ // 2, LH)), dma((2, NZ // 2, LH)),
-            dma((2, NZ)), dma((2, NY, LH)), dma((2, NY)),
-            dma((2, NZ // 2, LH)), dma((2, NZ // 2, LH)), dma((2, NZ // 2)), dma((2, NZ // 2)), dma((2, LH)),
+            dma((6, HK)), dma((6, HK)), dma((2, GROUPS)), dma((2, NZ // 2, GROUPS)), dma((2, NZ // 2, GROUPS)),
+            dma((2, NZ)), dma((2, NY, GROUPS)), dma((2, NY)),
+            dma((2, NZ // 2, GROUPS)), dma((2, NZ // 2, GROUPS)), dma((2, NZ // 2)), dma((2, NZ // 2)), dma((2, 2, NZ)),
             dma((HK,)), dma((2 * NX,)), dma, dma((6, 2 * PARTS)), dma((6, 2 * PARTS)), dma((2, PARTS)),
         ],
         compiler_params=pltpu.CompilerParams(

time: 94.5 us -> 90.8 us (0.961)
  the two profiles are of different devices: /device:TPU:1 before, /device:TPU:2 now
where the time goes in v5:
time: 90.8 us; the launch traced here: 90.6 us
  Pallas kernels  88.9 us (98%)
  local copies, waits for them, and re-layouts  1.66 us (2%)
    pallas_call x1, Pallas kernels, layer(): pl.pallas_call(layer_kernel, out_shape=jax.ShapeDtypeStruct((TOK, width),...  88.9 us

profile of v5, /device:TPU:2, one launch (start us, length us, event | category | flops | bytes accessed | tf_op | source)
XLA Modules:
  0.0 90.6 jit_solution(8227559581732375431)
XLA Ops:
  0.0 88.9 %layer.1 = bf16[320,384]{1,0:T(8,128)(2,1)} custom-call(s32[4]{0:T(128)} %owners_ref.1, s32[1,6]{1,0:T(1,128)} %pattern_ref.1, bf16[320,384]{1,0:T(8,128)(2,1)} %q_hbm.1, bf16[320,384]{1,0:T(8,128)(2,1)} %k_hbm.1, bf16[320,384]{1,0:T(8,128)(2,1)} %v_hbm.1, bf16[384,3072]{1,0:T(8,128)(2,1)} %w_hbm.1), custom_call_target="tpu_custom_call" | custom-call | tf_op jit(solution)/shard_map/layer/pallas_call | solution.py:566
  88.9 1.7 %copy.8 = bf16[320,384]{1,0:T(8,128)(2,1)} copy(bf16[320,384]{1,0:T(8,128)(2,1)} %layer.1) | data formatting | bytes 491520

commit v6 on v5

--- a/solution.py
+++ b/solution.py
@@ -28,15 +28,11 @@
 PER = HK // GROUPS
 PARTS = 2
 PACE = (
-    (("own", 2), ("spread",)),
-    (("own", 3),),
-    (("own", 4), ("here",), ("fixed", 0)),
-    (("own", 5), ("fixed", 1), ("on", 0), ("on", 1)),
-    (("fixed", 2), ("on", 2), ("on", 3), ("query",), ("near", 0)),
-    (("fixed", 3), ("on", 4)),
-    (("on", 5), ("near", 1)),
-    (("near", 2),),
-    (("fixed_part",),),
+    (("own", 2), ("own", 3), ("spread",)),
+    (("own", 4), ("own", 5), ("on", 0), ("here",), ("fixed", 0)),
+    (("on", 1), ("on", 2), ("fixed", 1), ("on", 3), ("query",), ("near", 0), ("fixed", 2)),
+    (("on", 4), ("on", 5), ("fixed", 3), ("near", 1)),
+    (("near", 2), ("fixed_part",)),
     (),
 )
 VMEM = pl.BlockSpec(memory_space=pltpu.VMEM)
@@ -46,9 +42,9 @@
 
 def layer_kernel(
     owners_ref, pattern_ref, q_hbm, k_hbm, v_hbm, w_hbm, out,
-    kv, qb, wb, mine, msend, mrecv, ps, pr, ss, sr, ysend, yr,
+    kv, qb, wb, mine, msend, mrecv, part_s, part_r, ysend, yr,
     scores, att, acc1, top1, total1, p, r1p, r1m, t2p, t2m, r2p, r2m, ty, ry,
-    hs_sem, hr_sem, m_sem, p_sem, s_sem, x_sem, y_sem, ys_sem, a_sem, b_sem, fa_sem, fb_sem, f_sem,
+    hs_sem, hr_sem, m_sem, p_sem, x_sem, y_sem, ys_sem, a_sem, fa_sem, fb_sem, f_sem,
     in_sem, w_sem, q_sem, mix_s, mix_r, c_sem,
 ):
     s = lax.axis_index("seq")
@@ -84,6 +80,8 @@
     far, near = NZ // 2, NZ // 2 - 1
     ahead = at(py, pz + 1)
     behind = at(py, pz - 1)
+    ahead2 = at(py, pz + 2)
+    behind2 = at(py, pz - 2)
 
     loads = []
     for h in range(LH):
@@ -140,11 +138,20 @@
     def swap(g):
         return remote(planes(msend, g), planes(mrecv, g), m_sem.at[0, g], m_sem.at[1, g], partner)
 
-    def p_copy(j, g):
-        return remote(ps.at[j, g], pr.at[j, g], p_sem.at[0, j, g], p_sem.at[1, j, g], ahead)
-
-    def s_copy(j, g):
-        return remote(ss.at[j, g], sr.at[j, g], s_sem.at[0, j, g], s_sem.at[1, j, g], behind)
+    def mine_at(q):
+        return mine.at[:, pl.ds(pl.multiple_of(lax.rem(q + NZ, NZ) * PIECE, PIECE), PIECE)]
+
+    def rs_copy(i):
+        src, dst, peer = (
+            (mine_at(pz + 3), part_r.at[1], ahead2),
+            (mine_at(pz - 3), part_r.at[2], behind2),
+            (mine_at(pz + 4), part_r.at[0], ahead2),
+            (mine_at(pz - 2), part_r.at[3], behind2),
+            (part_s.at[0], part_r.at[4], ahead2),
+            (part_s.at[1], part_r.at[5], ahead),
+            (part_s.at[2], part_r.at[6], behind),
+        )[i]
+        return remote(src, dst, p_sem.at[0, i], p_sem.at[1, i], peer)
 
     base = core * REF
 
@@ -172,21 +179,19 @@
     def y_fixed(d):
         return remote(fixed_rows(pz), fixed_rows(pz), ys_sem.at[0, d], ys_sem.at[1, 0], at(py + d, pz))
 
-    def around(j, g):
-        part = piece(g, pz - j)
-        return remote(part, part, a_sem.at[0, j, g], a_sem.at[1, j, g], ahead)
-
-    def around_arrived(j, g):
-        part = piece(g, pz - j - 1)
-        remote(part, part, a_sem.at[0, j, g], a_sem.at[1, j, g], ahead).wait_recv()
-
-    def back(j, g):
-        part = piece(g, pz + j)
-        return remote(part, part, b_sem.at[0, j, g], b_sem.at[1, j, g], behind)
-
-    def back_arrived(j, g):
-        part = piece(g, pz + j + 1)
-        remote(part, part, b_sem.at[0, j, g], b_sem.at[1, j, g], behind).wait_recv()
+    routes = ((0, 1), (0, -1), (0, 2), (0, -2), (-1, 2), (1, -2), (-2, 2))
+
+    def ag_copy(i):
+        off, to = routes[i]
+        part = piece(0, pz + off)
+        peer = {1: ahead, -1: behind, 2: ahead2, -2: behind2}[to]
+        return remote(part, part, a_sem.at[0, i], a_sem.at[1, i], peer)
+
+    def ag_arrived(i):
+        off, to = routes[i]
+        part = piece(0, pz + off - to)
+        remote(part, part, a_sem.at[0, i], a_sem.at[1, i], ahead).wait_recv()
+        share(0, off - to).start()
 
     def fixed_around(j):
         part = fixed_rows(pz - j)
@@ -350,6 +355,11 @@
         "own": halo_start, "on": halo_forward, "near": near_part, "spread": fixed_spread,
         "here": fixed_here, "fixed": fixed_start, "fixed_part": fixed_part, "query": query_load.wait,
     }
+
+    def pace(i):
+        for action in PACE[i]:
+            step_actions[action[0]](*action[1:])
+
     for g in groups:
         swap(g).start()
 
@@ -364,66 +374,41 @@
     query_load.start()
     for load in weight_loads:
         load.start()
-    for j in range(far):
-        for g in groups:
-            if j == 0:
-                swap(g).wait_recv()
-                mine[PER * g : PER * g + PER] = mine[PER * g : PER * g + PER] + mrecv[PER * g : PER * g + PER]
-                ps[0, g] = mine_rows(g, pz + far)
-                p_copy(0, g).start()
-                if near > 0:
-                    ss[0, g] = mine_rows(g, pz - near)
-                    s_copy(0, g).start()
-            else:
-                p_copy(j - 1, g).wait_recv()
-                ps[j, g] = mine_rows(g, pz + far - j) + pr[j - 1, g]
-                p_copy(j, g).start()
-                if j < near:
-                    s_copy(j - 1, g).wait_recv()
-                    ss[j, g] = mine_rows(g, pz - near + j) + sr[j - 1, g]
-                    s_copy(j, g).start()
-        for action in PACE[j]:
-            step_actions[action[0]](*action[1:])
-    for g in groups:
-        total = mine_rows(g, pz)
-        if near > 0:
-            s_copy(near - 1, g).wait_recv()
-            total = total + sr[near - 1, g]
-        p_copy(far - 1, g).wait_recv()
-        ysend[PER * g : PER * g + PER] = total + pr[far - 1, g]
-        for d in range(1, NY):
-            y_copy(d, g).start()
-    for action in PACE[far]:
-        step_actions[action[0]](*action[1:])
-    for g in groups:
-        total = ysend[PER * g : PER * g + PER]
-        for d in range(1, NY):
-            y_copy(d, g).wait_recv()
-            total = total + yr[d - 1, g]
-        piece(g, pz)[...] = total
-        around(0, g).start()
-        if near > 0:
-            back(0, g).start()
-        share(0, 0).start()
-    for action in PACE[far + 1]:
-        step_actions[action[0]](*action[1:])
-    for j in range(1, far):
-        for g in groups:
-            around_arrived(j - 1, g)
-            around(j, g).start()
-            share(0, -j).start()
-            if j <= near:
-                back_arrived(j - 1, g)
-                share(0, j).start()
-            if j < near:
-                back(j, g).start()
-        for action in PACE[far + 1 + j]:
-            step_actions[action[0]](*action[1:])
-    for g in groups:
-        around_arrived(far - 1, g)
-        share(0, -far).start()
-    for action in PACE[2 * far + 1]:
-        step_actions[action[0]](*action[1:])
+    swap(0).wait_recv()
+    mine[...] = mine[...] + mrecv[...]
+    for i in range(4):
+        rs_copy(i).start()
+    pace(0)
+    for i, first, held in ((5, 0, 1), (6, 1, 2), (4, 2, 0)):
+        rs_copy(first).wait_recv()
+        part_s[i - 4] = mine_rows(0, (pz + 2, pz + 1, pz - 1)[i - 4]) + part_r[held]
+        rs_copy(i).start()
+    pace(1)
+    total = mine_rows(0, pz)
+    for i, held in ((3, 3), (5, 5), (6, 6), (4, 4)):
+        rs_copy(i).wait_recv()
+        total = total + part_r[held]
+    ysend[...] = total
+    for d in range(1, NY):
+        y_copy(d, 0).start()
+    pace(2)
+    total = ysend[...]
+    for d in range(1, NY):
+        y_copy(d, 0).wait_recv()
+        total = total + yr[d - 1, 0]
+    piece(0, pz)[...] = total
+    for i in range(4):
+        ag_copy(i).start()
+    share(0, 0).start()
+    pace(3)
+    for i, onward in ((0, 4), (1, 5), (2, 6), (3, None)):
+        ag_arrived(i)
+        if onward is not None:
+            ag_copy(onward).start()
+    pace(4)
+    for i in (4, 5, 6):
+        ag_arrived(i)
+    pace(5)
     shared(0)
     for h in heads:
         last_part(h)
@@ -525,12 +510,9 @@
             share(kind, off).wait_send()
     for g in groups:
         swap(g).wait_send()
-        for j in range(far):
-            p_copy(j, g).wait_send()
-            around(j, g).wait_send()
-        for j in range(near):
-            s_copy(j, g).wait_send()
-            back(j, g).wait_send()
+        for i in range(7):
+            rs_copy(i).wait_send()
+            ag_copy(i).wait_send()
         for d in range(1, NY):
             y_copy(d, g).wait_send()
     for j in range(far):
@@ -556,7 +538,6 @@
     dma = pltpu.SemaphoreType.DMA
     width = LH * HD
     whole = pltpu.VMEM((HK, REF, HD), BF)
-    hop = pltpu.VMEM((NZ // 2, GROUPS, PER, PIECE, HD), BF)
     part = TOK // PARTS
     halves = pltpu.VMEM((2 * PARTS, part // 2, width), BF)
     fulls = pltpu.VMEM((2 * PARTS, part, width), BF)
@@ -571,15 +552,16 @@
         scratch_shapes=[
             pltpu.VMEM((HK, PAD, HD), BF), pltpu.VMEM((TOK, width), BF),
             pltpu.VMEM((2 * NX, width, width), BF),
-            whole, whole, whole, hop, hop, hop, hop,
+            whole, whole, whole,
+            pltpu.VMEM((3, HK, PIECE, HD), BF), pltpu.VMEM((7, HK, PIECE, HD), BF),
             pltpu.VMEM((HK, PIECE, HD), BF), pltpu.VMEM((NY - 1, GROUPS, PER, PIECE, HD), BF),
             pltpu.VMEM((TOK, PAD - OWN), jnp.float32), pltpu.VMEM((TOK, width), BF),
             pltpu.VMEM((LH, TOK, HD), jnp.float32), column, column,
             pltpu.VMEM((2 * NX, TOK, width), BF),
             halves, halves, halves, halves, fulls, fulls, pairs, pairs,
-            dma((6, HK)), dma((6, HK)), dma((2, GROUPS)), dma((2, NZ // 2, GROUPS)), dma((2, NZ // 2, GROUPS)),
+            dma((6, HK)), dma((6, HK)), dma((2, GROUPS)), dma((2, 7)),
             dma((2, NZ)), dma((2, NY, GROUPS)), dma((2, NY)),
-            dma((2, NZ // 2, GROUPS)), dma((2, NZ // 2, GROUPS)), dma((2, NZ // 2)), dma((2, NZ // 2)), dma((2, 2, NZ)),
+            dma((2, 7)), dma((2, NZ // 2)), dma((2, NZ // 2)), dma((2, 2, NZ)),
             dma((HK,)), dma((2 * NX,)), dma, dma((6, 2 * PARTS)), dma((6, 2 * PARTS)), dma((2, PARTS)),
         ],
         compiler_params=pltpu.CompilerParams(

time: 90.8 us -> 92.9 us (1.023)
  the two profiles are of different devices: /device:TPU:2 before, /device:TPU:64 now
where the time goes in v6:
time: 92.9 us; the launch traced here: 92.7 us
  Pallas kernels  91 us (98%)
  local copies, waits for them, and re-layouts  1.66 us (2%)
    pallas_call x1, Pallas kernels, layer(): pl.pallas_call(layer_kernel, out_shape=jax.ShapeDtypeStruct((TOK, width),...  91 us

profile of v6, /device:TPU:64, one launch (start us, length us, event | category | flops | bytes accessed | tf_op | source)
XLA Modules:
  0.0 92.7 jit_solution(6665636589321672601)
XLA Ops:
  0.0 91.0 %layer.1 = bf16[320,384]{1,0:T(8,128)(2,1)} custom-call(s32[4]{0:T(128)} %owners_ref.1, s32[1,6]{1,0:T(1,128)} %pattern_ref.1, bf16[320,384]{1,0:T(8,128)(2,1)} %q_hbm.1, bf16[320,384]{1,0:T(8,128)(2,1)} %k_hbm.1, bf16[320,384]{1,0:T(8,128)(2,1)} %v_hbm.1, bf16[384,3072]{1,0:T(8,128)(2,1)} %w_hbm.1), custom_call_target="tpu_custom_call" | custom-call | tf_op jit(solution)/shard_map/layer/pallas_call | solution.py:547
  91.0 1.7 %copy.8 = bf16[320,384]{1,0:T(8,128)(2,1)} copy(bf16[320,384]{1,0:T(8,128)(2,1)} %layer.1) | data formatting | bytes 491520

commit v7 on v5

--- a/solution.py
+++ b/solution.py
@@ -1,4 +1,4 @@
-import functools
+import math
 
 import jax
 import jax.numpy as jnp
@@ -46,7 +46,7 @@
 
 def layer_kernel(
     owners_ref, pattern_ref, q_hbm, k_hbm, v_hbm, w_hbm, out,
-    kv, qb, wb, mine, msend, mrecv, ps, pr, ss, sr, ysend, yr,
+    kv, qb, q2, wb, mine, msend, mrecv, ps, pr, ss, sr, ysend, yr,
     scores, att, acc1, top1, total1, p, r1p, r1m, t2p, t2m, r2p, r2m, ty, ry,
     hs_sem, hr_sem, m_sem, p_sem, s_sem, x_sem, y_sem, ys_sem, a_sem, b_sem, fa_sem, fb_sem, f_sem,
     in_sem, w_sem, q_sem, mix_s, mix_r, c_sem,
@@ -286,19 +286,19 @@
         edge = HALO + col * TOK
         closed = jnp.where(pattern_ref[0, col] != 0, 0.0, NEG)
         bias = bias + jnp.where((position >= edge) & (position < edge + TOK), closed, 0.0)
-    scale = HD ** -0.5
+    scale = HD ** -0.5 * math.log2(math.e)
 
     def segment(h, first, last):
-        q = qb[:, h * HD : (h + 1) * HD]
+        q = q2[h]
         peak = jnp.full((TOK, HD), NEG, jnp.float32)
         tiles = range(first, last, TILE)
         for row in tiles:
+            keys = kv[2 * h, row : row + TILE, :]
             sc = lax.dot_general(
-                q, kv[2 * h, row : row + TILE, :], (((1,), (1,)), ((), ())),
+                q, jnp.concatenate([keys, keys], axis=1), (((1,), (1,)), ((), ())),
                 preferred_element_type=jnp.float32,
             )
-            sc = sc * scale
-            if row >= OWN:
+            if row + TILE > HALO:
                 sc = sc + bias[:, row - OWN : row - OWN + TILE]
             scores[:, row - first : row - first + TILE] = sc
             peak = jnp.maximum(peak, jnp.maximum(sc[:, :HD], sc[:, HD:]))
@@ -306,12 +306,20 @@
         total = jnp.zeros((TOK, HD), jnp.float32)
         acc = jnp.zeros((TOK, HD), jnp.float32)
         for row in tiles:
-            w = jnp.exp(scores[:, row - first : row - first + TILE] - top)
+            w = jnp.exp2(scores[:, row - first : row - first + TILE] - top)
             total = total + (w[:, :HD] + w[:, HD:])
             acc = acc + jnp.dot(
                 w.astype(BF), kv[2 * h + 1, row : row + TILE, :], preferred_element_type=jnp.float32
             )
         return top, jnp.sum(total, axis=1, keepdims=True), acc
+
+    def scale_queries():
+        query_load.wait()
+        for h in range(LH):
+            exact = qb[:, h * HD : (h + 1) * HD].astype(jnp.float32) * scale
+            upper = exact.astype(BF)
+            q2[h, :, :HD] = upper
+            q2[h, :, HD:] = (exact - upper.astype(jnp.float32)).astype(BF)
 
     def near_part(h):
         for col in range(2 * REACH):
@@ -326,8 +334,8 @@
     def joined(h, first, last):
         top, total, acc = segment(h, first, last)
         best = jnp.maximum(top, top1[h])
-        new = jnp.exp(top - best)
-        old = jnp.exp(top1[h] - best)
+        new = jnp.exp2(top - best)
+        old = jnp.exp2(top1[h] - best)
         return best, total * new + total1[h] * old, acc * new + acc1[h] * old
 
     def fixed_part():
@@ -348,7 +356,7 @@
     groups = range(GROUPS)
     step_actions = {
         "own": halo_start, "on": halo_forward, "near": near_part, "spread": fixed_spread,
-        "here": fixed_here, "fixed": fixed_start, "fixed_part": fixed_part, "query": query_load.wait,
+        "here": fixed_here, "fixed": fixed_start, "fixed_part": fixed_part, "query": scale_queries,
     }
     for g in groups:
         swap(g).start()
@@ -509,17 +517,6 @@
     project(x * 2 + side)
     for i in range(PARTS, 2 * PARTS):
         pass_on(i)
-    for c in range(PARTS):
-        total = collect(PARTS + c)
-        cross(c).wait_recv()
-        out[c * part : (c + 1) * part, :] = (total + ry[c].astype(jnp.float32)).astype(BF)
-
-    for i in range(2 * PARTS):
-        for copy in first[i] + direct[i] + second[i]:
-            copy.wait_send()
-    for c in range(PARTS):
-        cross(c).wait_send()
-
     for kind in range(2):
         for off in range(-far, near + 1):
             share(kind, off).wait_send()
@@ -550,6 +547,16 @@
     def _():
         for q in range(1, NZ):
             fixed_copy(q).wait_send()
+    for c in range(PARTS):
+        total = collect(PARTS + c)
+        cross(c).wait_recv()
+        out[c * part : (c + 1) * part, :] = (total + ry[c].astype(jnp.float32)).astype(BF)
+
+    for i in range(2 * PARTS):
+        for copy in first[i] + direct[i] + second[i]:
+            copy.wait_send()
+    for c in range(PARTS):
+        cross(c).wait_send()
 
 
 def layer(owners, pattern, q, k, v, w):
@@ -570,6 +577,7 @@
         out_specs=VMEM,
         scratch_shapes=[
             pltpu.VMEM((HK, PAD, HD), BF), pltpu.VMEM((TOK, width), BF),
+            pltpu.VMEM((LH, TOK, 2 * HD), BF),
             pltpu.VMEM((2 * NX, width, width), BF),
             whole, whole, whole, hop, hop, hop, hop,
             pltpu.VMEM((HK, PIECE, HD), BF), pltpu.VMEM((NY - 1, GROUPS, PER, PIECE, HD), BF),

time: 90.8 us -> 90.7 us (level)
  no operation moved by 1% of the time
where the time goes in v7:
time: 90.7 us; the launch traced here: 90.5 us
  Pallas kernels  88.8 us (98%)
  local copies, waits for them, and re-layouts  1.66 us (2%)
    pallas_call x1, Pallas kernels, layer(): pl.pallas_call(layer_kernel, out_shape=jax.ShapeDtypeStruct((TOK, width),...  88.8 us

profile of v7, /device:TPU:2, one launch (start us, length us, event | category | flops | bytes accessed | tf_op | source)
XLA Modules:
  0.0 90.5 jit_solution(8032340082433868409)
XLA Ops:
  0.0 88.8 %layer.1 = bf16[320,384]{1,0:T(8,128)(2,1)} custom-call(s32[4]{0:T(128)} %owners_ref.1, s32[1,6]{1,0:T(1,128)} %pattern_ref.1, bf16[320,384]{1,0:T(8,128)(2,1)} %q_hbm.1, bf16[320,384]{1,0:T(8,128)(2,1)} %k_hbm.1, bf16[320,384]{1,0:T(8,128)(2,1)} %v_hbm.1, bf16[384,3072]{1,0:T(8,128)(2,1)} %w_hbm.1), custom_call_target="tpu_custom_call" | custom-call | tf_op jit(solution)/shard_map/layer/pallas_call | solution.py:573
  88.8 1.7 %copy.8 = bf16[320,384]{1,0:T(8,128)(2,1)} copy(bf16[320,384]{1,0:T(8,128)(2,1)} %layer.1) | data formatting | bytes 491520

commit v8 on v7

--- a/solution.py
+++ b/solution.py
@@ -288,9 +288,9 @@
         bias = bias + jnp.where((position >= edge) & (position < edge + TOK), closed, 0.0)
     scale = HD ** -0.5 * math.log2(math.e)
 
-    def segment(h, first, last):
-        q = q2[h]
-        peak = jnp.full((TOK, HD), NEG, jnp.float32)
+    def segment(h, first, last, low=0, high=TOK):
+        q = q2[h, low:high]
+        peak = jnp.full((high - low, HD), NEG, jnp.float32)
         tiles = range(first, last, TILE)
         for row in tiles:
             keys = kv[2 * h, row : row + TILE, :]
@@ -300,13 +300,13 @@
             )
             if row + TILE > HALO:
                 sc = sc + bias[:, row - OWN : row - OWN + TILE]
-            scores[:, row - first : row - first + TILE] = sc
+            scores[low:high, row - first : row - first + TILE] = sc
             peak = jnp.maximum(peak, jnp.maximum(sc[:, :HD], sc[:, HD:]))
         top = jnp.max(peak, axis=1, keepdims=True)
-        total = jnp.zeros((TOK, HD), jnp.float32)
-        acc = jnp.zeros((TOK, HD), jnp.float32)
+        total = jnp.zeros((high - low, HD), jnp.float32)
+        acc = jnp.zeros((high - low, HD), jnp.float32)
         for row in tiles:
-            w = jnp.exp2(scores[:, row - first : row - first + TILE] - top)
+            w = jnp.exp2(scores[low:high, row - first : row - first + TILE] - top)
             total = total + (w[:, :HD] + w[:, HD:])
             acc = acc + jnp.dot(
                 w.astype(BF), kv[2 * h + 1, row : row + TILE, :], preferred_element_type=jnp.float32
@@ -331,12 +331,13 @@
         total1[h] = total
         acc1[h] = acc
 
-    def joined(h, first, last):
-        top, total, acc = segment(h, first, last)
-        best = jnp.maximum(top, top1[h])
+    def joined(h, first, last, low=0, high=TOK):
+        top, total, acc = segment(h, first, last, low, high)
+        before = top1[h, low:high]
+        best = jnp.maximum(top, before)
         new = jnp.exp2(top - best)
-        old = jnp.exp2(top1[h] - best)
-        return best, total * new + total1[h] * old, acc * new + acc1[h] * old
+        old = jnp.exp2(before - best)
+        return best, total * new + total1[h, low:high] * old, acc * new + acc1[h, low:high] * old
 
     def fixed_part():
         fixed_finish()
@@ -347,9 +348,10 @@
             total1[h] = total
             acc1[h] = acc
 
-    def last_part(h):
-        best, total, acc = joined(h, 0, 2 * REF)
-        att[:, h * HD : (h + 1) * HD] = (acc / total).astype(BF)
+    def last_part(low, high):
+        for h in range(LH):
+            best, total, acc = joined(h, 0, 2 * REF, low, high)
+            att[low:high, h * HD : (h + 1) * HD] = (acc / total).astype(BF)
 
     source = (pz == 0) & (py == 0)
     heads = range(LH)
@@ -433,13 +435,13 @@
     for action in PACE[2 * far + 1]:
         step_actions[action[0]](*action[1:])
     shared(0)
-    for h in heads:
-        last_part(h)
     for load in weight_loads:
         load.wait()
 
-    def project(b):
-        p[b] = jnp.dot(att[...], wb[b], preferred_element_type=jnp.float32).astype(BF)
+    def project(b, low=0, high=TOK):
+        p[b, low:high] = jnp.dot(
+            att[low:high], wb[b], preferred_element_type=jnp.float32
+        ).astype(BF)
 
     def head_copy(kind, i, src, dst, peer):
         return pltpu.make_async_remote_copy(
@@ -493,24 +495,30 @@
             + r2m[i].astype(jnp.float32)
         )
 
-    def launch(phase):
-        which = items[phase * PARTS][0]
-        todo = range(phase * PARTS, (phase + 1) * PARTS)
-        project(xo * 2 + which)
-        for i in todo:
-            for copy in first[i]:
-                copy.start()
-        project(xn * 2 + which)
-        project(xp * 2 + which)
-        for i in todo:
-            for copy in direct[i]:
-                copy.start()
-
-    launch(0)
-    for i in range(PARTS):
-        pass_on(i)
-    launch(1)
-    project(x * 2 + 1 - side)
+    def begin(copies):
+        for copy in copies:
+            copy.start()
+
+    other = 1 - side
+    for c in range(PARTS):
+        span = (c * part, (c + 1) * part)
+        last_part(*span)
+        project(xo * 2 + other, *span)
+        begin(first[c])
+        if c > 0:
+            pass_on(c - 1)
+        project(xn * 2 + other, *span)
+        project(xp * 2 + other, *span)
+        begin(direct[c])
+    project(xo * 2 + side)
+    for i in range(PARTS, 2 * PARTS):
+        begin(first[i])
+    pass_on(PARTS - 1)
+    project(xn * 2 + side)
+    project(xp * 2 + side)
+    for i in range(PARTS, 2 * PARTS):
+        begin(direct[i])
+    project(x * 2 + other)
     for c in range(PARTS):
         ty[c] = collect(c).astype(BF)
         cross(c).start()

time: 90.7 us -> 87.1 us (0.960)
  the two profiles are of different devices: /device:TPU:2 before, /device:TPU:1 now
where the time goes in v8:
time: 87.1 us; the launch traced here: 85.5 us
  Pallas kernels  83.8 us (96%)
  local copies, waits for them, and re-layouts  1.66 us (2%)
    pallas_call x1, Pallas kernels, layer(): pl.pallas_call(layer_kernel, out_shape=jax.ShapeDtypeStruct((TOK, width),...  83.8 us

profile of v8, /device:TPU:1, one launch (start us, length us, event | category | flops | bytes accessed | tf_op | source)
XLA Modules:
  0.0 85.5 jit_solution(16194799698776191908)
XLA Ops:
  0.0 83.8 %layer.1 = bf16[320,384]{1,0:T(8,128)(2,1)} custom-call(s32[4]{0:T(128)} %owners_ref.1, s32[1,6]{1,0:T(1,128)} %pattern_ref.1, bf16[320,384]{1,0:T(8,128)(2,1)} %q_hbm.1, bf16[320,384]{1,0:T(8,128)(2,1)} %k_hbm.1, bf16[320,384]{1,0:T(8,128)(2,1)} %v_hbm.1, bf16[384,3072]{1,0:T(8,128)(2,1)} %w_hbm.1), custom_call_target="tpu_custom_call" | custom-call | tf_op jit(solution)/shard_map/layer/pallas_call | solution.py:581
  83.8 1.7 %copy.8 = bf16[320,384]{1,0:T(8,128)(2,1)} copy(bf16[320,384]{1,0:T(8,128)(2,1)} %layer.1) | data formatting | bytes 491520

commit v9 on v8

--- a/solution.py
+++ b/solution.py
@@ -510,16 +510,18 @@
         project(xn * 2 + other, *span)
         project(xp * 2 + other, *span)
         begin(direct[c])
+    project(x * 2 + other)
     project(xo * 2 + side)
     for i in range(PARTS, 2 * PARTS):
         begin(first[i])
     pass_on(PARTS - 1)
+    ty[0] = collect(0).astype(BF)
+    cross(0).start()
     project(xn * 2 + side)
     project(xp * 2 + side)
     for i in range(PARTS, 2 * PARTS):
         begin(direct[i])
-    project(x * 2 + other)
-    for c in range(PARTS):
+    for c in range(1, PARTS):
         ty[c] = collect(c).astype(BF)
         cross(c).start()
     project(x * 2 + side)

time: 87.1 us -> 87.1 us (level)
  no operation moved by 1% of the time
where the time goes in v9:
time: 87.1 us; the launch traced here: 85.5 us
  Pallas kernels  83.8 us (96%)
  local copies, waits for them, and re-layouts  1.66 us (2%)
    pallas_call x1, Pallas kernels, layer(): pl.pallas_call(layer_kernel, out_shape=jax.ShapeDtypeStruct((TOK, width),...  83.8 us

profile of v9, /device:TPU:1, one launch (start us, length us, event | category | flops | bytes accessed | tf_op | source)
XLA Modules:
  0.0 85.5 jit_solution(5223812645614379901)
XLA Ops:
  0.0 83.8 %layer.1 = bf16[320,384]{1,0:T(8,128)(2,1)} custom-call(s32[4]{0:T(128)} %owners_ref.1, s32[1,6]{1,0:T(1,128)} %pattern_ref.1, bf16[320,384]{1,0:T(8,128)(2,1)} %q_hbm.1, bf16[320,384]{1,0:T(8,128)(2,1)} %k_hbm.1, bf16[320,384]{1,0:T(8,128)(2,1)} %v_hbm.1, bf16[384,3072]{1,0:T(8,128)(2,1)} %w_hbm.1), custom_call_target="tpu_custom_call" | custom-call | tf_op jit(solution)/shard_map/layer/pallas_call | solution.py:583
  83.8 1.7 %copy.8 = bf16[320,384]{1,0:T(8,128)(2,1)} copy(bf16[320,384]{1,0:T(8,128)(2,1)} %layer.1) | data formatting | bytes 491520

commit v10 on v9

--- a/solution.py
+++ b/solution.py
@@ -30,14 +30,14 @@
 PACE = (
     (("own", 2), ("spread",)),
     (("own", 3),),
-    (("own", 4), ("here",), ("fixed", 0)),
-    (("own", 5), ("fixed", 1), ("on", 0), ("on", 1)),
-    (("fixed", 2), ("on", 2), ("on", 3), ("query",), ("near", 0)),
-    (("fixed", 3), ("on", 4)),
-    (("on", 5), ("near", 1)),
+    (("own", 4),),
+    (("own", 5), ("here",), ("fixed", 0), ("on", 0)),
+    (("on", 1), ("on", 2), ("on", 3), ("fixed", 1), ("query",), ("near", 0)),
+    (("fixed", 2), ("on", 4)),
+    (("on", 5), ("fixed", 3)),
+    (("near", 1),),
     (("near", 2),),
     (("fixed_part",),),
-    (),
 )
 VMEM = pl.BlockSpec(memory_space=pltpu.VMEM)
 SMEM = pl.BlockSpec(memory_space=pltpu.SMEM)

time: 87.1 us -> 90.3 us (1.037)
  Pallas kernels: 83.8 us -> 87.8 us
    pallas_call x1, Pallas kernels: 83.8 us -> 87.8 us  [layer(): pl.pallas_call(layer_kernel, out_shape=jax.ShapeDtypeStruct((TOK, width),...]
where the time goes in v10:
time: 90.3 us; the launch traced here: 89.5 us
  Pallas kernels  87.8 us (97%)
  local copies, waits for them, and re-layouts  1.66 us (2%)
    pallas_call x1, Pallas kernels, layer(): pl.pallas_call(layer_kernel, out_shape=jax.ShapeDtypeStruct((TOK, width),...  87.8 us

profile of v10, /device:TPU:1, one launch (start us, length us, event | category | flops | bytes accessed | tf_op | source)
XLA Modules:
  0.0 89.5 jit_solution(10789961944954154352)
XLA Ops:
  0.0 87.8 %layer.1 = bf16[320,384]{1,0:T(8,128)(2,1)} custom-call(s32[4]{0:T(128)} %owners_ref.1, s32[1,6]{1,0:T(1,128)} %pattern_ref.1, bf16[320,384]{1,0:T(8,128)(2,1)} %q_hbm.1, bf16[320,384]{1,0:T(8,128)(2,1)} %k_hbm.1, bf16[320,384]{1,0:T(8,128)(2,1)} %v_hbm.1, bf16[384,3072]{1,0:T(8,128)(2,1)} %w_hbm.1), custom_call_target="tpu_custom_call" | custom-call | tf_op jit(solution)/shard_map/layer/pallas_call | solution.py:583
  87.8 1.7 %copy.8 = bf16[320,384]{1,0:T(8,128)(2,1)} copy(bf16[320,384]{1,0:T(8,128)(2,1)} %layer.1) | data formatting | bytes 491520

commit v11 on v9

--- a/solution.py
+++ b/solution.py
@@ -35,8 +35,8 @@
     (("fixed", 2), ("on", 2), ("on", 3), ("query",), ("near", 0)),
     (("fixed", 3), ("on", 4)),
     (("on", 5), ("near", 1)),
-    (("near", 2),),
-    (("fixed_part",),),
+    (("near", 2), ("fixed_part",)),
+    (),
     (),
 )
 VMEM = pl.BlockSpec(memory_space=pltpu.VMEM)

time: 87.1 us -> 91.9 us (1.055); the launches traced: 85.5 us -> 91.7 us
  Pallas kernels: 83.8 us -> 90 us
    pallas_call x1, Pallas kernels: 83.8 us -> 90 us  [layer(): pl.pallas_call(layer_kernel, out_shape=jax.ShapeDtypeStruct((TOK, width),...]
where the time goes in v11:
time: 91.9 us; the launch traced here: 91.7 us
  Pallas kernels  90 us (98%)
  local copies, waits for them, and re-layouts  1.66 us (2%)
    pallas_call x1, Pallas kernels, layer(): pl.pallas_call(layer_kernel, out_shape=jax.ShapeDtypeStruct((TOK, width),...  90 us

profile of v11, /device:TPU:1, one launch (start us, length us, event | category | flops | bytes accessed | tf_op | source)
XLA Modules:
  0.0 91.7 jit_solution(1993951990936124798)
XLA Ops:
  0.0 90.0 %layer.1 = bf16[320,384]{1,0:T(8,128)(2,1)} custom-call(s32[4]{0:T(128)} %owners_ref.1, s32[1,6]{1,0:T(1,128)} %pattern_ref.1, bf16[320,384]{1,0:T(8,128)(2,1)} %q_hbm.1, bf16[320,384]{1,0:T(8,128)(2,1)} %k_hbm.1, bf16[320,384]{1,0:T(8,128)(2,1)} %v_hbm.1, bf16[384,3072]{1,0:T(8,128)(2,1)} %w_hbm.1), custom_call_target="tpu_custom_call" | custom-call | tf_op jit(solution)/shard_map/layer/pallas_call | solution.py:583
  90.0 1.7 %copy.8 = bf16[320,384]{1,0:T(8,128)(2,1)} copy(bf16[320,384]{1,0:T(8,128)(2,1)} %layer.1) | data formatting | bytes 491520
